TPU v7x, 32 devices: a whole 2x2x4 slice. The times are simulated.
32 devices in a mesh: dp: 4 (over y, x), row: 8 (over z, core).
Axes of the slice: x: 2, y: 2, z: 4, core: 2. Of those that a mesh axis runs over, the one named last changes fastest.
Arguments:
- frames: bfloat16 [16, 64, 64, 256], P('dp', 'row'), may hold values from -6 to 6
- tokens: bfloat16 [32, 1024, 768], P(('dp', 'row')), may hold values from -6 to 6
- segment_ids: int32 [32, 1024], P(('dp', 'row')), may hold values from 0 to 3, never falling along the last dimension, each value on 1 to 512 neighbouring positions
- clip_frame: int32 [32, 4], P(('dp', 'row')), may hold values from 0 to 3
- filter_weight: bfloat16 [9, 256, 256], replicated, may hold values from -0.125 to 0.125
- filter_bias: float32 [256], replicated, may hold values from -0.5 to 0.5
- context_gain: float32 [256], replicated, may hold values from 0.5 to 1.5
- context_shift: float32 [256], replicated, may hold values from -0.25 to 0.25
- cross_query: bfloat16 [768, 768], replicated, may hold values from -0.21875 to 0.21875
- cross_key: bfloat16 [256, 768], replicated, may hold values from -1.5 to 1.5
- cross_value: bfloat16 [256, 768], replicated, may hold values from -1.5 to 1.5
- cross_output: bfloat16 [768, 768], replicated, may hold values from -0.875 to 0.875
- first_gain: float32 [768], replicated, may hold values from 0.5 to 1.5
- first_shift: float32 [768], replicated, may hold values from -0.625 to 0.625
- self_project: bfloat16 [768, 2304], replicated, may hold values from -0.3125 to 0.3125
- self_output: bfloat16 [768, 768], replicated, may hold values from -0.875 to 0.875
- second_gain: float32 [768], replicated, may hold values from 0.5 to 1.5
- second_shift: float32 [768], replicated, may hold values from -1.75 to 1.75
- up_weight: bfloat16 [768, 3072], replicated, may hold values from -0.21875 to 0.21875
- up_bias: float32 [3072], replicated, may hold values from -3 to 3
- down_weight: bfloat16 [3072, 768], replicated, may hold values from -0.109375 to 0.109375
- cotangent: bfloat16 [32, 1024, 768], P(('dp', 'row')), may hold values from -6 to 6
Outputs:
- middle: float32 [32, 1024, 768], P(('dp', 'row'))
- output: float32 [32, 1024, 768], P(('dp', 'row'))
- tokens_grad: float32 [32, 1024, 768], P(('dp', 'row'))
- frames_grad: float32 [16, 64, 64, 256], P('dp', 'row')
- filter_weight_grad: float32 [9, 256, 256], P(None, None, 'row')
- filter_bias_grad: float32 [256], P('row')
- context_gain_grad: float32 [256], P('row')
- context_shift_grad: float32 [256], P('row')
- cross_query_grad: float32 [768, 768], P(None, 'row')
- cross_key_grad: float32 [256, 768], P(None, 'row')
- cross_value_grad: float32 [256, 768], P(None, 'row')
- cross_output_grad: float32 [768, 768], P(None, 'row')
- first_gain_grad: float32 [768], P('row')
- first_shift_grad: float32 [768], P('row')
- self_project_grad: float32 [768, 2304], P(None, 'row')
- self_output_grad: float32 [768, 768], P(None, 'row')
- second_gain_grad: float32 [768], P('row')
- second_shift_grad: float32 [768], P('row')
- up_weight_grad: float32 [768, 3072], P(None, 'row')
- up_bias_grad: float32 [3072], P('row')
- down_weight_grad: float32 [3072, 768], P(None, 'row')
Inputs may be any that keep to these rules, and one draw needn't show every extreme that they name: `segment_ids`: ids never fall along a row; each of the 4 clips of a row holds 1 to 512 tokens, and one clip of every row holds exactly 512. Clip c of token row r reads context frame (r // 8) * 4 + clip_frame[r, c].
All inputs are finite; a program needn't handle non-finite values.
Results may differ from a plain program's by a relative error of at most 0.03.
Values may be sent and summed in bfloat16 or wider, within the bound.
A program may use at most 384 MiB of HBM per device.

v0:
```python
import math

import jax
import jax.numpy as jnp
from jax import lax
from jax.sharding import PartitionSpec as P

D = 768
H = 12
HD = 64
FF = 3072
C = 256
IMG = 64
POOL = 4
CLIPS = 4
SEQ = 1024
SEQ_DEV = 1
KEYS = 256


epsilon = 1e-05
negative = -1e30


def extended(cells, sides, width):
    for axis, dim in sides:
        count = lax.axis_size(axis)
        ends = count - 1
        head = lax.slice_in_dim(cells, 0, width, axis=dim)
        tail = lax.slice_in_dim(cells, cells.shape[dim] - width, cells.shape[dim], axis=dim)
        cells = jnp.concatenate(
            [
                lax.ppermute(tail, axis, [(i, (i + 1) % count) for i in range(ends)]),
                cells,
                lax.ppermute(head, axis, [((i + 1) % count, i) for i in range(ends)]),
            ],
            axis=dim,
        )
    return cells


def layer_norm(values, gain, shift):
    average = jnp.mean(values, -1, keepdims=True)
    centred = values - average
    variance = jnp.mean(centred * centred, -1, keepdims=True)
    return centred * lax.rsqrt(variance + epsilon) * gain + shift


def norm_back(values, gain, shift, grad):
    _, pullback = jax.vjp(layer_norm, values, gain, shift)
    return pullback(grad)


def gelu_back(values, grad):
    _, pullback = jax.vjp(jax.nn.gelu, values)
    return pullback(grad)[0]


def fast_dot(left, right):
    return jnp.dot(left, right, preferred_element_type=jnp.float32)


def split_heads(matrix):
    return matrix.reshape(matrix.shape[0], H, HD)


def block_scores(query_block, key_rows):
    score_scale = 1.0 / math.sqrt(HD)
    return (
        jnp.einsum(
            "qhd,khd->hqk",
            split_heads(query_block),
            split_heads(key_rows),
            preferred_element_type=jnp.float32,
        )
        * score_scale
    )


def attend_forward(queries, key_rows, value_rows, mask_of):
    block_rows = min(512, queries.shape[0])

    def one_block(first_row):
        query_block = lax.dynamic_slice_in_dim(queries, first_row, block_rows, 0)
        scores = jnp.where(
            mask_of(first_row, block_rows)[None], block_scores(query_block, key_rows), negative
        )
        highest = jnp.max(scores, -1, keepdims=True)
        weights_exp = jnp.exp(scores - highest)
        summed = jnp.sum(weights_exp, -1, keepdims=True)
        softmax_probs = (weights_exp / summed).astype(jnp.bfloat16)
        attended = jnp.einsum(
            "hqk,khd->qhd",
            softmax_probs,
            split_heads(value_rows),
            preferred_element_type=jnp.float32,
        )
        return (
            attended.reshape(block_rows, D).astype(jnp.bfloat16),
            (highest + jnp.log(summed))[:, :, 0],
        )

    firsts = jnp.arange(queries.shape[0] // block_rows, dtype=jnp.int32) * block_rows
    attended, log_sums = lax.map(one_block, firsts)
    return (attended.reshape(-1, D), log_sums)


def attend_backward(queries, key_rows, value_rows, mixed_grad, log_sums, mask_of):
    block_rows = min(512, queries.shape[0])
    score_scale = 1.0 / math.sqrt(HD)

    def one_block(running, inputs):
        first_row, block_sums = inputs
        query_block = lax.dynamic_slice_in_dim(queries, first_row, block_rows, 0)
        grad_block = lax.dynamic_slice_in_dim(mixed_grad, first_row, block_rows, 0)
        scores = jnp.where(
            mask_of(first_row, block_rows)[None], block_scores(query_block, key_rows), negative
        )
        softmax_probs = jnp.exp(scores - block_sums[:, :, None])
        grad_heads = split_heads(grad_block)
        prob_grad = jnp.einsum(
            "qhd,khd->hqk", grad_heads, split_heads(value_rows), preferred_element_type=jnp.float32
        )
        row_dot = jnp.sum(softmax_probs * prob_grad, -1, keepdims=True)
        score_grad = (softmax_probs * (prob_grad - row_dot)).astype(jnp.bfloat16)
        query_grad = (
            jnp.einsum(
                "hqk,khd->qhd",
                score_grad,
                split_heads(key_rows),
                preferred_element_type=jnp.float32,
            )
            * score_scale
        )
        key_grad = (
            jnp.einsum(
                "hqk,qhd->khd",
                score_grad,
                split_heads(query_block),
                preferred_element_type=jnp.float32,
            )
            * score_scale
        )
        value_grad = jnp.einsum(
            "hqk,qhd->khd",
            softmax_probs.astype(jnp.bfloat16),
            grad_heads,
            preferred_element_type=jnp.float32,
        )
        running = (running[0] + key_grad.reshape(-1, D), running[1] + value_grad.reshape(-1, D))
        return (running, query_grad.reshape(block_rows, D))

    firsts = jnp.arange(queries.shape[0] // block_rows, dtype=jnp.int32) * block_rows
    zero_keys = jnp.zeros((key_rows.shape[0], D), jnp.float32)
    (key_grad, value_grad), query_grad = lax.scan(
        one_block, (zero_keys, zero_keys), (firsts, log_sums)
    )
    return (query_grad.reshape(-1, D), key_grad, value_grad)


def cross_mask(row_frames, key_frames):

    def cross_allowed(first_row, row_count):
        block_frames = lax.dynamic_slice_in_dim(row_frames, first_row, row_count, 0)
        return block_frames[:, None] == key_frames[None, :]

    return cross_allowed


def causal_mask(row_segments):
    positions = jnp.arange(row_segments.shape[0], dtype=jnp.int32)

    def causal_allowed(first_row, row_count):
        query_positions = first_row + jnp.arange(row_count, dtype=jnp.int32)
        block_segments = lax.dynamic_slice_in_dim(row_segments, first_row, row_count, 0)
        return (query_positions[:, None] >= positions[None, :]) & (
            block_segments[:, None] == row_segments[None, :]
        )

    return causal_allowed


def convolve(padded, taps, rows_here):
    summed = jnp.zeros((padded.shape[0], rows_here, IMG, taps.shape[2]), jnp.float32)
    for kernel_tap in range(9):
        row_shift = kernel_tap // 3
        col_shift = kernel_tap % 3
        window = padded[:, row_shift : row_shift + rows_here, col_shift : col_shift + IMG, :]
        summed = summed + jnp.einsum(
            "fyxc,cd->fyxd", window, taps[kernel_tap], preferred_element_type=jnp.float32
        )
    return summed


def filter_grads(padded, pre_grad, rows_here):
    return jnp.stack(
        [
            jnp.einsum(
                "fyxc,fyxd->cd",
                padded[
                    :,
                    kernel_tap // 3 : kernel_tap // 3 + rows_here,
                    kernel_tap % 3 : kernel_tap % 3 + IMG,
                    :,
                ],
                pre_grad,
                preferred_element_type=jnp.float32,
            )
            for kernel_tap in range(9)
        ]
    )


def on_device(
    frames,
    tokens,
    segment_ids,
    clip_frame,
    filter_weight,
    filter_bias,
    context_gain,
    context_shift,
    cross_query,
    cross_key,
    cross_value,
    cross_output,
    first_gain,
    first_shift,
    self_project,
    self_output,
    second_gain,
    second_shift,
    up_weight,
    up_bias,
    down_weight,
    cotangent,
):
    frame_count = frames.shape[0]
    rows_here = frames.shape[1]
    padded = extended(frames, (("row", 1),), 1)
    padded = jnp.pad(padded, ((0, 0), (0, 0), (1, 1), (0, 0)))
    pre_act = convolve(padded, filter_weight, rows_here) + filter_bias
    activated = jax.nn.gelu(pre_act)
    normed = layer_norm(activated, context_gain, context_shift)
    pooled = jnp.mean(
        normed.reshape(frame_count, rows_here // POOL, POOL, IMG // POOL, POOL, C), axis=(2, 4)
    )
    pooled = pooled.reshape(frame_count, -1, C).astype(jnp.bfloat16)
    local_keys = jnp.einsum(
        "fkc,cd->fkd", pooled, cross_key, preferred_element_type=jnp.float32
    ).astype(jnp.bfloat16)
    local_values = jnp.einsum(
        "fkc,cd->fkd", pooled, cross_value, preferred_element_type=jnp.float32
    ).astype(jnp.bfloat16)
    all_keys, all_values = (
        lax.all_gather(local_keys, "row", axis=1, tiled=True),
        lax.all_gather(local_values, "row", axis=1, tiled=True),
    )
    key_flat = all_keys.reshape(-1, D)
    value_flat = all_values.reshape(-1, D)
    key_frames = jnp.arange(key_flat.shape[0], dtype=jnp.int32) // KEYS
    flat_tokens = tokens.reshape(-1, D)
    cross_q = fast_dot(flat_tokens, cross_query).astype(jnp.bfloat16).reshape(SEQ_DEV, SEQ, D)
    clip_range = jnp.arange(CLIPS, dtype=jnp.int32)
    frame_ids = jnp.sum(
        jnp.where(segment_ids[:, :, None] == clip_range[None, None, :], clip_frame[:, None, :], 0),
        axis=2,
    )

    def cross_row(inputs):
        row_queries, row_frames = inputs
        return attend_forward(row_queries, key_flat, value_flat, cross_mask(row_frames, key_frames))

    cross_mixed, cross_sums = lax.map(cross_row, (cross_q, frame_ids))
    cross_flat = cross_mixed.reshape(-1, D)
    middle = flat_tokens.astype(jnp.float32) + fast_dot(cross_flat, cross_output)
    first_normed = layer_norm(middle, first_gain, first_shift).astype(jnp.bfloat16)
    packed = fast_dot(first_normed, self_project).astype(jnp.bfloat16).reshape(SEQ_DEV, SEQ, 3 * D)

    def self_row(inputs):
        row_packed, row_segments = inputs
        return attend_forward(
            row_packed[:, :D],
            row_packed[:, D : 2 * D],
            row_packed[:, 2 * D :],
            causal_mask(row_segments),
        )

    self_mixed, self_sums = lax.map(self_row, (packed, segment_ids))
    self_flat = self_mixed.reshape(-1, D)
    second_mid = middle + fast_dot(self_flat, self_output)
    second_normed = layer_norm(second_mid, second_gain, second_shift).astype(jnp.bfloat16)
    hidden_pre = fast_dot(second_normed, up_weight) + up_bias
    hidden = jax.nn.gelu(hidden_pre).astype(jnp.bfloat16)
    output = second_mid + fast_dot(hidden, down_weight)
    out_grad = cotangent.reshape(-1, D)
    down_weight_grad = fast_dot(hidden.T, out_grad)
    hidden_grad = fast_dot(out_grad, down_weight.T)
    pre_grad = gelu_back(hidden_pre, hidden_grad).astype(jnp.bfloat16)
    up_weight_grad = fast_dot(second_normed.T, pre_grad)
    up_bias_grad = jnp.sum(pre_grad.astype(jnp.float32), 0)
    normed_back = fast_dot(pre_grad, up_weight.T)
    mid_part, second_gain_grad, second_shift_grad = norm_back(
        second_mid, second_gain, second_shift, normed_back
    )
    second_grad = out_grad.astype(jnp.float32) + mid_part
    attn_grad = second_grad.astype(jnp.bfloat16)
    self_output_grad = fast_dot(self_flat.T, attn_grad)
    self_mixed_grad = (
        fast_dot(attn_grad, self_output.T).astype(jnp.bfloat16).reshape(SEQ_DEV, SEQ, D)
    )

    def self_back(inputs):
        row_packed, row_segments, row_grad, row_sums = inputs
        query_grad, key_grad, value_grad = attend_backward(
            row_packed[:, :D],
            row_packed[:, D : 2 * D],
            row_packed[:, 2 * D :],
            row_grad,
            row_sums,
            causal_mask(row_segments),
        )
        return jnp.concatenate([query_grad, key_grad, value_grad], -1).astype(jnp.bfloat16)

    packed_grad = lax.map(self_back, (packed, segment_ids, self_mixed_grad, self_sums)).reshape(
        -1, 3 * D
    )
    self_project_grad = fast_dot(first_normed.T, packed_grad)
    first_back = fast_dot(packed_grad, self_project.T)
    mid_part, first_gain_grad, first_shift_grad = norm_back(
        middle, first_gain, first_shift, first_back
    )
    middle_grad = second_grad + mid_part
    cross_proj_grad = middle_grad.astype(jnp.bfloat16)
    cross_output_grad = fast_dot(cross_flat.T, cross_proj_grad)
    cross_mixed_grad = (
        fast_dot(cross_proj_grad, cross_output.T).astype(jnp.bfloat16).reshape(SEQ_DEV, SEQ, D)
    )

    def cross_back(running, inputs):
        row_queries, row_frames, row_grad, row_sums = inputs
        query_grad, key_grad, value_grad = attend_backward(
            row_queries,
            key_flat,
            value_flat,
            row_grad,
            row_sums,
            cross_mask(row_frames, key_frames),
        )
        return ((running[0] + key_grad, running[1] + value_grad), query_grad)

    zero_keys = jnp.zeros(key_flat.shape, jnp.float32)
    (context_key_grad, context_value_grad), cross_q_grad = lax.scan(
        cross_back, (zero_keys, zero_keys), (cross_q, frame_ids, cross_mixed_grad, cross_sums)
    )
    query_low = cross_q_grad.reshape(-1, D).astype(jnp.bfloat16)
    cross_query_grad = fast_dot(flat_tokens.T, query_low)
    tokens_grad = middle_grad + fast_dot(query_low, cross_query.T)
    context_key_grad = context_key_grad.reshape(frame_count, -1, D)
    context_value_grad = context_value_grad.reshape(frame_count, -1, D)
    key_exact = cross_key.astype(jnp.float32)
    value_exact = cross_value.astype(jnp.float32)
    highest_prec = lax.Precision.HIGHEST
    own_key_grad, own_value_grad = (
        lax.psum_scatter(
            context_key_grad.astype(jnp.bfloat16), "row", scatter_dimension=1, tiled=True
        ).astype(jnp.float32),
        lax.psum_scatter(
            context_value_grad.astype(jnp.bfloat16), "row", scatter_dimension=1, tiled=True
        ).astype(jnp.float32),
    )
    pooled_exact = pooled.astype(jnp.float32)
    cross_key_grad = jnp.einsum("fkc,fkd->cd", pooled_exact, own_key_grad, precision=highest_prec)
    cross_value_grad = jnp.einsum(
        "fkc,fkd->cd", pooled_exact, own_value_grad, precision=highest_prec
    )
    pooled_grad = jnp.einsum(
        "fkd,cd->fkc", own_key_grad, key_exact, precision=highest_prec
    ) + jnp.einsum("fkd,cd->fkc", own_value_grad, value_exact, precision=highest_prec)
    spread_grad = pooled_grad.reshape(frame_count, rows_here // POOL, 1, IMG // POOL, 1, C) / (
        POOL * POOL
    )
    spread_grad = jnp.broadcast_to(
        spread_grad, (frame_count, rows_here // POOL, POOL, IMG // POOL, POOL, C)
    )
    spread_grad = spread_grad.reshape(frame_count, rows_here, IMG, C)
    activated_grad, context_gain_grad, context_shift_grad = norm_back(
        activated, context_gain, context_shift, spread_grad
    )
    filter_pre_grad = gelu_back(pre_act, activated_grad).astype(jnp.bfloat16)
    filter_bias_grad = jnp.sum(filter_pre_grad.astype(jnp.float32), (0, 1, 2))
    filter_weight_grad = filter_grads(padded, filter_pre_grad, rows_here)
    grad_padded = extended(filter_pre_grad, (("row", 1),), 1)
    grad_padded = jnp.pad(grad_padded, ((0, 0), (0, 0), (1, 1), (0, 0)))
    flipped = jnp.transpose(filter_weight[::-1], (0, 2, 1))
    frames_grad = convolve(grad_padded, flipped, rows_here)
    shares = (
        lax.psum_scatter(
            filter_weight_grad.reshape(9 * C, C).astype(jnp.bfloat16),
            "row",
            scatter_dimension=1,
            tiled=True,
        ).astype(jnp.float32),
        lax.psum_scatter(
            filter_bias_grad.reshape(1, C).astype(jnp.bfloat16),
            "row",
            scatter_dimension=1,
            tiled=True,
        ).astype(jnp.float32),
        lax.psum_scatter(
            context_gain_grad.reshape(1, C).astype(jnp.bfloat16),
            "row",
            scatter_dimension=1,
            tiled=True,
        ).astype(jnp.float32),
        lax.psum_scatter(
            context_shift_grad.reshape(1, C).astype(jnp.bfloat16),
            "row",
            scatter_dimension=1,
            tiled=True,
        ).astype(jnp.float32),
        lax.psum_scatter(
            cross_query_grad.astype(jnp.bfloat16), "row", scatter_dimension=1, tiled=True
        ).astype(jnp.float32),
        lax.psum_scatter(
            cross_key_grad.astype(jnp.bfloat16), "row", scatter_dimension=1, tiled=True
        ).astype(jnp.float32),
        lax.psum_scatter(
            cross_value_grad.astype(jnp.bfloat16), "row", scatter_dimension=1, tiled=True
        ).astype(jnp.float32),
        lax.psum_scatter(
            cross_output_grad.astype(jnp.bfloat16), "row", scatter_dimension=1, tiled=True
        ).astype(jnp.float32),
        lax.psum_scatter(
            first_gain_grad.reshape(1, D).astype(jnp.bfloat16),
            "row",
            scatter_dimension=1,
            tiled=True,
        ).astype(jnp.float32),
        lax.psum_scatter(
            first_shift_grad.reshape(1, D).astype(jnp.bfloat16),
            "row",
            scatter_dimension=1,
            tiled=True,
        ).astype(jnp.float32),
        lax.psum_scatter(
            self_project_grad.astype(jnp.bfloat16), "row", scatter_dimension=1, tiled=True
        ).astype(jnp.float32),
        lax.psum_scatter(
            self_output_grad.astype(jnp.bfloat16), "row", scatter_dimension=1, tiled=True
        ).astype(jnp.float32),
        lax.psum_scatter(
            second_gain_grad.reshape(1, D).astype(jnp.bfloat16),
            "row",
            scatter_dimension=1,
            tiled=True,
        ).astype(jnp.float32),
        lax.psum_scatter(
            second_shift_grad.reshape(1, D).astype(jnp.bfloat16),
            "row",
            scatter_dimension=1,
            tiled=True,
        ).astype(jnp.float32),
        lax.psum_scatter(
            up_weight_grad.astype(jnp.bfloat16), "row", scatter_dimension=1, tiled=True
        ).astype(jnp.float32),
        lax.psum_scatter(
            up_bias_grad.reshape(1, FF).astype(jnp.bfloat16), "row", scatter_dimension=1, tiled=True
        ).astype(jnp.float32),
        lax.psum_scatter(
            down_weight_grad.astype(jnp.bfloat16), "row", scatter_dimension=1, tiled=True
        ).astype(jnp.float32),
    )
    shares = tuple(
        (
            lax.psum(shares[0].astype(jnp.bfloat16), "dp").astype(jnp.float32),
            lax.psum(shares[1].astype(jnp.bfloat16), "dp").astype(jnp.float32),
            lax.psum(shares[2].astype(jnp.bfloat16), "dp").astype(jnp.float32),
            lax.psum(shares[3].astype(jnp.bfloat16), "dp").astype(jnp.float32),
            lax.psum(shares[4].astype(jnp.bfloat16), "dp").astype(jnp.float32),
            lax.psum(shares[5].astype(jnp.bfloat16), "dp").astype(jnp.float32),
            lax.psum(shares[6].astype(jnp.bfloat16), "dp").astype(jnp.float32),
            lax.psum(shares[7].astype(jnp.bfloat16), "dp").astype(jnp.float32),
            lax.psum(shares[8].astype(jnp.bfloat16), "dp").astype(jnp.float32),
            lax.psum(shares[9].astype(jnp.bfloat16), "dp").astype(jnp.float32),
            lax.psum(shares[10].astype(jnp.bfloat16), "dp").astype(jnp.float32),
            lax.psum(shares[11].astype(jnp.bfloat16), "dp").astype(jnp.float32),
            lax.psum(shares[12].astype(jnp.bfloat16), "dp").astype(jnp.float32),
            lax.psum(shares[13].astype(jnp.bfloat16), "dp").astype(jnp.float32),
            lax.psum(shares[14].astype(jnp.bfloat16), "dp").astype(jnp.float32),
            lax.psum(shares[15].astype(jnp.bfloat16), "dp").astype(jnp.float32),
            lax.psum(shares[16].astype(jnp.bfloat16), "dp").astype(jnp.float32),
        )
    )
    return (
        middle.reshape(SEQ_DEV, SEQ, D),
        output.reshape(SEQ_DEV, SEQ, D),
        tokens_grad.reshape(SEQ_DEV, SEQ, D),
        frames_grad,
        shares[0].reshape(9, C, -1),
        shares[1].reshape(-1),
        shares[2].reshape(-1),
        shares[3].reshape(-1),
        shares[4],
        shares[5],
        shares[6],
        shares[7],
        shares[8].reshape(-1),
        shares[9].reshape(-1),
        shares[10],
        shares[11],
        shares[12].reshape(-1),
        shares[13].reshape(-1),
        shares[14],
        shares[15].reshape(-1),
        shares[16],
    )


def solution(mesh):
    in_specs = (
        P("dp", "row", None, None),
        P(("dp", "row"), None, None),
        P(("dp", "row"), None),
        P(("dp", "row"), None),
        P(),
        P(),
        P(),
        P(),
        P(),
        P(),
        P(),
        P(),
        P(),
        P(),
        P(),
        P(),
        P(),
        P(),
        P(),
        P(),
        P(),
        P(("dp", "row"), None, None),
    )
    out_specs = (
        P(("dp", "row"), None, None),
        P(("dp", "row"), None, None),
        P(("dp", "row"), None, None),
        P("dp", "row", None, None),
        P(None, None, "row"),
        P("row"),
        P("row"),
        P("row"),
        P(None, "row"),
        P(None, "row"),
        P(None, "row"),
        P(None, "row"),
        P("row"),
        P("row"),
        P(None, "row"),
        P(None, "row"),
        P("row"),
        P("row"),
        P(None, "row"),
        P("row"),
        P(None, "row"),
    )
    return jax.shard_map(
        on_device, mesh=mesh, in_specs=in_specs, out_specs=out_specs, check_vma=False
    )
```

profile of v0, /device:TPU:0, one launch (start us, length us, event | category | flops | bytes accessed | tf_op | source)
XLA Modules:
  0.0 1632.6 jit_solution(13925951275094146176)
XLA Ops:
  51.4 14.1 all-gather.3.cloned.1.call-done
  76.9 15.4 all-gather.5.cloned.1.call-done
  105.5 88.8 %while.98 = (s32[]{:T(128)}, bf16[2,512,768]{2,1,0:T(8,128)(2,1)}, f32[2,12,512]{2,1,0:T(8,128)}, s32[2]{0:T(128)S(1)}, s32[1024]{0:T(1024)S(1)}, /*index=5*/bf1...) while((s32[]{:T(128)}, bf16[2,512,768]{2,1,0:T(8,128)(2,1)}, ...), condition=%wide.wide.region_7.8_spmd.clone, body=%wide.wide.region_4.7_spmd.clone.sunk | while | flops 1687029760 | bytes 200907088 | solution.py:104
  110.1 10.7 fusion.343
  120.8 12.3 fusion.344
  154.3 10.7 fusion.343
  165.0 12.3 fusion.344
  215.7 90.3 %while.96 = (s32[]{:T(128)}, bf16[2,512,768]{2,1,0:T(8,128)(2,1)}, f32[2,12,512]{2,1,0:T(8,128)}, s32[2]{0:T(128)S(1)}, s32[1024]{0:T(1024)S(1)}, /*index=5*/bf1...) while((s32[]{:T(128)}, bf16[2,512,768]{2,1,0:T(8,128)(2,1)}, ...), condition=%wide.region_13.14_spmd.clone, body=%wide.region_10.13_spmd.clone.sunk | while | flops 1688070656 | bytes 200907088 | solution.py:104
  221.1 10.7 fusion.324
  231.9 12.3 fusion.325
  266.2 10.7 fusion.324
  276.9 12.3 fusion.325
  318.3 18.5 %fusion.191 = (bf16[3072]{0:T(1024)(128)(2,1)}, bf16[1024,3072]{1,0:T(8,128)(2,1)}) fusion(f32[1024,3072]{1,0:T(8,128)S(1)} %fusion.179, f32[3072]{0:T(1024)S(1)} %copy-done.116, bf16[3072,768]{1,0:T(8,128)(2,1)} %param.50, bf16[1,1024,768]{2,1,0:T(8,128)(2,1)S(1)} %copy-done.59), kind=kOutput, calls=%fused_computation.323 | convolution fusion | flops 4901041152 | bytes 25184256 | tf_op jit(solution)/shard_map/dot_general | solution.py:60
  336.9 10.3 fusion.190
  362.5 210.2 %while.97 = (s32[]{:T(128)}, f32[1024,768]{0,1:T(8,128)}, f32[1024,768]{0,1:T(8,128)}, bf16[2,512,768]{2,1,0:T(8,128)(2,1)}, s32[2]{0:T(128)S(1)}, /*index=5*/bf...) while((s32[]{:T(128)}, f32[1024,768]{0,1:T(8,128)}, ...), condition=%wide.region_20.21_spmd.clone, body=%wide.region_18.20_spmd.clone.sunk | while | flops 4127189504 | bytes 310401536 | solution.py:155
  375.7 10.2 fusion.337
  385.9 13.2 fusion.339
  399.1 18.8 %multiply_reduce_fusion.14 = (f32[12,512]{1,0:T(8,128)}, f32[12,512,1024]{2,1,0:T(8,128)}) fusion(f32[12,512,1024]{2,1,0:T(8,128)} %fusion.337, f32[12,512]{1,0:T(8,128)} %dynamic-slice_bitcast_fusion.5, pred[512,1024]{1,0:T(8,128)(4,1)} %fusion.338, bf16[512,12,64]{0,2,1:T(8,128)(2,1)} %bitcast.611, bf16[1024,12,64]{0,2,1:T(8,128)(2,1)} %bitcast.616), kind=kOutput, calls=%fused_computation.40.clone.1 | convolution fusion | flops 836757504 | bytes 53264384 | tf_op jit(solution)/shard_map/while/body/eval_jaxpr/while/body/eval_jaxpr/qhd,khd->hqk/dot_general | solution.py:121
  417.9 22.2 %multiply_convert_fusion.9 = bf16[12,512,1024]{2,1,0:T(8,128)(2,1)} fusion(f32[12,512,1024]{2,1,0:T(8,128)} %get-tuple-element.1156, f32[12,512,1024]{2,1,0:T(8,128)} %fusion.337, f32[12,512]{1,0:T(8,128)} %get-tuple-element.1157, f32[12,512]{1,0:T(8,128)} %dynamic-slice_bitcast_fusion.5, pred[512,1024]{1,0:T(8,128)(4,1)} %fusion.338), kind=kLoop, calls=%fused_computation.39.clone.1 | loop fusion | flops 37748736 | bytes 63488000 | tf_op jit(solution)/shard_map/while/body/eval_jaxpr/while/body/eval_jaxpr/convert_element_type | solution.py:125
  490.7 13.2 fusion.339
  503.9 18.8 %multiply_reduce_fusion.14 = (f32[12,512]{1,0:T(8,128)}, f32[12,512,1024]{2,1,0:T(8,128)}) fusion(f32[12,512,1024]{2,1,0:T(8,128)} %fusion.337, f32[12,512]{1,0:T(8,128)} %dynamic-slice_bitcast_fusion.5, pred[512,1024]{1,0:T(8,128)(4,1)} %fusion.338, bf16[512,12,64]{0,2,1:T(8,128)(2,1)} %bitcast.611, bf16[1024,12,64]{0,2,1:T(8,128)(2,1)} %bitcast.616), kind=kOutput, calls=%fused_computation.40.clone.1 | convolution fusion | flops 836757504 | bytes 53264384 | tf_op jit(solution)/shard_map/while/body/eval_jaxpr/while/body/eval_jaxpr/qhd,khd->hqk/dot_general | solution.py:121
  522.7 22.2 %multiply_convert_fusion.9 = bf16[12,512,1024]{2,1,0:T(8,128)(2,1)} fusion(f32[12,512,1024]{2,1,0:T(8,128)} %get-tuple-element.1156, f32[12,512,1024]{2,1,0:T(8,128)} %fusion.337, f32[12,512]{1,0:T(8,128)} %get-tuple-element.1157, f32[12,512]{1,0:T(8,128)} %dynamic-slice_bitcast_fusion.5, pred[512,1024]{1,0:T(8,128)(4,1)} %fusion.338), kind=kLoop, calls=%fused_computation.39.clone.1 | loop fusion | flops 37748736 | bytes 63488000 | tf_op jit(solution)/shard_map/while/body/eval_jaxpr/while/body/eval_jaxpr/convert_element_type | solution.py:125
  603.5 208.4 %while.99 = (s32[]{:T(128)}, f32[1024,768]{0,1:T(8,128)}, f32[1024,768]{0,1:T(8,128)}, bf16[2,512,768]{2,1,0:T(8,128)(2,1)}, s32[2]{0:T(128)S(1)}, /*index=5*/bf...) while((s32[]{:T(128)}, f32[1024,768]{0,1:T(8,128)}, ...), condition=%wide.wide.region_25.26_spmd.clone, body=%wide.wide.region_23.25_spmd.clone.sunk | while | flops 4126148608 | bytes 310401536 | solution.py:155
  626.2 13.1 fusion.357
  639.2 18.8 %multiply_reduce_fusion.15 = (f32[12,512]{1,0:T(8,128)}, f32[12,512,1024]{2,1,0:T(8,128)}) fusion(f32[12,512,1024]{2,1,0:T(8,128)} %fusion.356, f32[12,512]{1,0:T(8,128)} %dynamic-slice_bitcast_fusion.6, pred[512,1024]{1,0:T(8,128)(4,1)} %broadcast_compare_fusion.7, bf16[512,12,64]{0,2,1:T(8,128)(2,1)} %bitcast.613, ...), kind=kOutput, calls=%fused_computation.59.clone.clone.1 | convolution fusion | flops 836757504 | bytes 53264384 | tf_op jit(solution)/shard_map/while/body/eval_jaxpr/while/body/eval_jaxpr/qhd,khd->hqk/dot_general | solution.py:121
  658.1 22.2 %multiply_convert_fusion.10 = bf16[12,512,1024]{2,1,0:T(8,128)(2,1)} fusion(f32[12,512,1024]{2,1,0:T(8,128)} %get-tuple-element.1185, f32[12,512,1024]{2,1,0:T(8,128)} %fusion.356, f32[12,512]{1,0:T(8,128)} %get-tuple-element.1186, f32[12,512]{1,0:T(8,128)} %dynamic-slice_bitcast_fusion.6, pred[512,1024]{1,0:T(8,128)(4,1)} %broadcast_compare_fusion.7), kind=kLoop, calls=%fused_computation.58.clone.clone.1 | loop fusion | flops 37748736 | bytes 63488000 | tf_op jit(solution)/shard_map/while/body/eval_jaxpr/while/body/eval_jaxpr/convert_element_type | solution.py:125
  730.1 13.1 fusion.357
  743.1 18.8 %multiply_reduce_fusion.15 = (f32[12,512]{1,0:T(8,128)}, f32[12,512,1024]{2,1,0:T(8,128)}) fusion(f32[12,512,1024]{2,1,0:T(8,128)} %fusion.356, f32[12,512]{1,0:T(8,128)} %dynamic-slice_bitcast_fusion.6, pred[512,1024]{1,0:T(8,128)(4,1)} %broadcast_compare_fusion.7, bf16[512,12,64]{0,2,1:T(8,128)(2,1)} %bitcast.613, ...), kind=kOutput, calls=%fused_computation.59.clone.clone.1 | convolution fusion | flops 836757504 | bytes 53264384 | tf_op jit(solution)/shard_map/while/body/eval_jaxpr/while/body/eval_jaxpr/qhd,khd->hqk/dot_general | solution.py:121
  762.0 22.2 %multiply_convert_fusion.10 = bf16[12,512,1024]{2,1,0:T(8,128)(2,1)} fusion(f32[12,512,1024]{2,1,0:T(8,128)} %get-tuple-element.1185, f32[12,512,1024]{2,1,0:T(8,128)} %fusion.356, f32[12,512]{1,0:T(8,128)} %get-tuple-element.1186, f32[12,512]{1,0:T(8,128)} %dynamic-slice_bitcast_fusion.6, pred[512,1024]{1,0:T(8,128)(4,1)} %broadcast_compare_fusion.7), kind=kLoop, calls=%fused_computation.58.clone.clone.1 | loop fusion | flops 37748736 | bytes 63488000 | tf_op jit(solution)/shard_map/while/body/eval_jaxpr/while/body/eval_jaxpr/convert_element_type | solution.py:125
  830.4 21.5 %reduce-scatter.38.cloned.1.call-done = bf16[4,32,768]{2,1,0:T(8,128)(2,1)} async-done(((bf16[4,256,768]{2,1,0:T(8,128)(2,1)}), bf16[4,32,768]{2,1,0:T(8,128)(2,1)}) %reduce-scatter.38.cloned.1.call-update) | async-done | bytes 196624 | tf_op jit(solution)/shard_map/reduce_scatter | solution.py:365
  853.9 32.5 %reduce-scatter.40.cloned.1.call-done = bf16[4,32,768]{2,1,0:T(8,128)(2,1)} async-done(((bf16[4,256,768]{2,1,0:T(8,128)(2,1)}), bf16[4,32,768]{2,1,0:T(8,128)(2,1)}) %reduce-scatter.40.cloned.1.call-update) | async-done | bytes 196624 | tf_op jit(solution)/shard_map/reduce_scatter | solution.py:368
  967.8 10.8 convolution_convert_fusion.1
  986.9 12.4 add_bitcast_fusion.1
  1017.5 26.3 %reduce-scatter.74.cloned.1.call-done = bf16[384,1]{1,0:T(8,128)(2,1)} async-done(((bf16[3072,1]{1,0:T(8,128)(2,1)}), bf16[384,1]{1,0:T(8,128)(2,1)}) %reduce-scatter.74.cloned.1.call-update) | async-done | bytes 784
  1053.3 21.2 %reduce-scatter.62.cloned.1.call-done = bf16[32,1]{1,0:T(8,128)(2,1)} async-done(((bf16[256,1]{1,0:T(8,128)(2,1)}), bf16[32,1]{1,0:T(8,128)(2,1)}) %reduce-scatter.62.cloned.1.call-update) | async-done | bytes 80
  1075.8 29.7 %reduce-scatter.58.cloned.1.call-done = bf16[32,1]{1,0:T(8,128)(2,1)} async-done(((bf16[256,1]{1,0:T(8,128)(2,1)}), bf16[32,1]{1,0:T(8,128)(2,1)}) %reduce-scatter.58.cloned.1.call-update) | async-done | bytes 80
  1106.8 29.7 %reduce-scatter.60.cloned.1.call-done = bf16[32,1]{1,0:T(8,128)(2,1)} async-done(((bf16[256,1]{1,0:T(8,128)(2,1)}), bf16[32,1]{1,0:T(8,128)(2,1)}) %reduce-scatter.60.cloned.1.call-update) | async-done | bytes 80
  1143.6 23.9 %reduce-scatter.46.cloned.1.call-done = bf16[256,96]{0,1:T(8,128)(2,1)} async-done(((bf16[256,768]{0,1:T(8,128)(2,1)}), bf16[256,96]{0,1:T(8,128)(2,1)}) %reduce-scatter.46.cloned.1.call-update) | async-done | bytes 49168 | tf_op jit(solution)/shard_map/reduce_scatter | solution.py:425
  1167.5 31.1 %reduce-scatter.48.cloned.1.call-done = bf16[256,96]{0,1:T(8,128)(2,1)} async-done(((bf16[256,768]{0,1:T(8,128)(2,1)}), bf16[256,96]{0,1:T(8,128)(2,1)}) %reduce-scatter.48.cloned.1.call-update) | async-done | bytes 49168 | tf_op jit(solution)/shard_map/reduce_scatter | solution.py:428
  1201.9 29.8 %reduce-scatter.42.cloned.1.call-done = bf16[2304,32]{0,1:T(8,128)(2,1)} async-done(((bf16[2304,256]{0,1:T(8,128)(2,1)}), bf16[2304,32]{0,1:T(8,128)(2,1)}) %reduce-scatter.42.cloned.1.call-update) | async-done | bytes 147472 | tf_op jit(solution)/shard_map/reduce_scatter | solution.py:398
  1233.4 53.7 %reduce-scatter.72.cloned.1.call-done = bf16[384,768]{1,0:T(8,128)(2,1)} async-done(((bf16[3072,768]{1,0:T(8,128)(2,1)}), bf16[384,768]{1,0:T(8,128)(2,1)}) %reduce-scatter.72.cloned.1.call-update) | async-done | bytes 589840
  1289.2 31.0 %reduce-scatter.54.cloned.1.call-done = bf16[768,96]{0,1:T(8,128)(2,1)} async-done(((bf16[768,768]{0,1:T(8,128)(2,1)}), bf16[768,96]{0,1:T(8,128)(2,1)}) %reduce-scatter.54.cloned.1.call-update) | async-done | bytes 147472 | tf_op jit(solution)/shard_map/reduce_scatter | solution.py:449
  1320.2 33.5 %reduce-scatter.50.cloned.1.call-done = bf16[768,96]{0,1:T(8,128)(2,1)} async-done(((bf16[768,768]{0,1:T(8,128)(2,1)}), bf16[768,96]{0,1:T(8,128)(2,1)}) %reduce-scatter.50.cloned.1.call-update) | async-done | bytes 147472 | tf_op jit(solution)/shard_map/reduce_scatter | solution.py:431
  1353.6 33.2 %reduce-scatter.44.cloned.1.call-done = bf16[768,96]{0,1:T(8,128)(2,1)} async-done(((bf16[768,768]{0,1:T(8,128)(2,1)}), bf16[768,96]{0,1:T(8,128)(2,1)}) %reduce-scatter.44.cloned.1.call-update) | async-done | bytes 147472 | tf_op jit(solution)/shard_map/reduce_scatter | solution.py:422
  1386.9 44.2 %reduce-scatter.52.cloned.1.call-done = bf16[768,288]{0,1:T(8,128)(2,1)} async-done(((bf16[768,2304]{0,1:T(8,128)(2,1)}), bf16[768,288]{0,1:T(8,128)(2,1)}) %reduce-scatter.52.cloned.1.call-update) | async-done | bytes 442384 | tf_op jit(solution)/shard_map/reduce_scatter | solution.py:446
  1431.0 55.9 %reduce-scatter.56.cloned.1.call-done = bf16[3072,96]{0,1:T(8,128)(2,1)} async-done(((bf16[3072,768]{0,1:T(8,128)(2,1)}), bf16[3072,96]{0,1:T(8,128)(2,1)}) %reduce-scatter.56.cloned.1.call-update) | async-done | bytes 589840 | tf_op jit(solution)/shard_map/reduce_scatter | solution.py:470
  1495.3 39.8 %all-reduce.7.cloned.1.call-done = (bf16[32]{0:T(256)(128)(2,1)}, bf16[32]{0:T(256)(128)(2,1)}, bf16[32]{0:T(256)(128)(2,1)}, bf16[256,96]{0,1:T(8,128)(2,1)}, b...) async-done(((bf16[32]{0:T(256)(128)(2,1)}, ...) | async-done | bytes 100048 | tf_op jit(solution)/shard_map/psum | solution.py:477
  1547.3 68.6 %all-reduce.9.cloned.1.call-done = (bf16[9,256,32]{1,0,2:T(8,128)(2,1)}, bf16[768,96]{0,1:T(8,128)(2,1)}, bf16[768,96]{0,1:T(8,128)(2,1)}, bf16[768,288]{0,1:T(8...) async-done(((bf16[9,256,32]{1,0,2:T(8,128)(2,1)}, bf16[768,96]{0,1:T(8,128)(2,1)}, bf16[768,96]{0,1:T(8,128)(2,1)}, ...) | async-done | bytes 2211856 | tf_op jit(solution)/shard_map/psum | solution.py:476
  (618 shorter events, 593.2 us)
Async XLA Ops:
  7.2 192.0 %copy-start = (bf16[768,2304]{1,0:T(8,128)(2,1)S(1)}, bf16[768,2304]{1,0:T(8,128)(2,1)}, u32[]{:S(2)}) copy-start(bf16[768,2304]{1,0:T(8,128)(2,1)} %param.44) | copy-start | bytes 10616836
  7.2 58.3 %all-gather.3.cloned.1.call-start = ((), (), s32[]{:S(2)}) async-start(), calls=%async_computation.19 | async-start | bytes 1769472 | tf_op jit(solution)/shard_map/all_gather | solution.py:256
  8.4 5.5 collective-permute-start
  10.9 5.4 collective-permute-start.1
  36.8 55.4 %all-gather.5.cloned.1.call-start = ((), (), s32[]{:S(2)}) async-start(), calls=%async_computation.20 | async-start | bytes 1769472 | tf_op jit(solution)/shard_map/all_gather | solution.py:257
  38.8 813.1 %reduce-scatter.38.cloned.1.call-start = ((), (), s32[]{:S(2)}) async-start(), calls=%async_computation.21 | async-start | bytes 1769472 | tf_op jit(solution)/shard_map/reduce_scatter | solution.py:365
  110.1 23.0 %copy-start.60 = (bf16[1024,12,64]{0,2,1:T(8,128)(2,1)S(1)}, bf16[1024,12,64]{0,2,1:T(8,128)(2,1)}, u32[]{:S(2)}) copy-start(bf16[1024,12,64]{0,2,1:T(8,128)(2,1)} %get-tuple-element.1223) | copy-start | bytes 4718596 | tf_op jit(solution)/shard_map/while/body/eval_jaxpr/while
  120.8 15.4 copy-start.1
  154.2 23.0 %copy-start.60 = (bf16[1024,12,64]{0,2,1:T(8,128)(2,1)S(1)}, bf16[1024,12,64]{0,2,1:T(8,128)(2,1)}, u32[]{:S(2)}) copy-start(bf16[1024,12,64]{0,2,1:T(8,128)(2,1)} %get-tuple-element.1223) | copy-start | bytes 4718596 | tf_op jit(solution)/shard_map/while/body/eval_jaxpr/while
  165.0 15.4 copy-start.1
  221.1 23.0 %copy-start.28 = (bf16[1024,768]{0,1:T(8,128)(2,1)S(1)}, bf16[1024,768]{0,1:T(8,128)(2,1)}, u32[]{:S(2)}) copy-start(bf16[1024,768]{0,1:T(8,128)(2,1)} %get-tuple-element.1257) | copy-start | bytes 4718596 | tf_op jit(solution)/shard_map/while/body/eval_jaxpr/while
  231.9 15.4 copy-start.2
  266.2 23.0 %copy-start.28 = (bf16[1024,768]{0,1:T(8,128)(2,1)S(1)}, bf16[1024,768]{0,1:T(8,128)(2,1)}, u32[]{:S(2)}) copy-start(bf16[1024,768]{0,1:T(8,128)(2,1)} %get-tuple-element.1257) | copy-start | bytes 4718596 | tf_op jit(solution)/shard_map/while/body/eval_jaxpr/while
  276.9 15.4 copy-start.2
  311.0 44.2 %copy-start.74 = (f32[1024]{0:T(1024)}, f32[1024]{0:T(1024)S(1)}, u32[]{:S(2)}) copy-start(f32[1024]{0:T(1024)S(1)} %broadcast_multiply_fusion.1) | copy-start | bytes 12292
  312.7 42.6 %copy-start.76 = (f32[1024]{0:T(1024)}, f32[1024]{0:T(1024)S(1)}, u32[]{:S(2)}) copy-start(f32[1024]{0:T(1024)S(1)} %fusion.173) | copy-start | bytes 12292
  318.3 18.6 %copy-start.45 = (f32[1024,3072]{1,0:T(8,128)}, f32[1024,3072]{1,0:T(8,128)S(1)}, u32[]{:S(2)}) copy-start(f32[1024,3072]{1,0:T(8,128)S(1)} %fusion.179) | copy-start | bytes 37748740
  375.6 10.2 copy-start.8
  375.7 10.2 copy-start.24
  375.7 10.2 copy-start.51
  480.4 10.2 copy-start.24
  480.5 10.2 copy-start.51
  615.9 10.2 copy-start.9
  615.9 10.2 copy-start.25
  615.9 10.2 copy-start.52
  719.9 10.2 copy-start.52
  817.9 68.5 %reduce-scatter.40.cloned.1.call-start = ((), (), s32[]{:S(2)}) async-start(), calls=%async_computation.22 | async-start | bytes 1769472 | tf_op jit(solution)/shard_map/reduce_scatter | solution.py:368
  823.8 188.4 %reduce-scatter.70.cloned.1.call-start = ((), (), s32[]{:S(2)}) async-start(), calls=%async_computation.37 | async-start | bytes 221184
  825.4 188.1 %reduce-scatter.68.cloned.1.call-start = ((), (), s32[]{:S(2)}) async-start(), calls=%async_computation.36 | async-start | bytes 221184
  826.4 188.5 %reduce-scatter.66.cloned.1.call-start = ((), (), s32[]{:S(2)}) async-start(), calls=%async_computation.35 | async-start | bytes 221184
  828.0 188.2 %reduce-scatter.64.cloned.1.call-start = ((), (), s32[]{:S(2)}) async-start(), calls=%async_computation.34 | async-start | bytes 221184
  828.9 214.9 %reduce-scatter.74.cloned.1.call-start = ((), (), s32[]{:S(2)}) async-start(), calls=%async_computation.39 | async-start | bytes 884736
  830.3 244.2 %reduce-scatter.62.cloned.1.call-start = ((), (), s32[]{:S(2)}) async-start(), calls=%async_computation.33 | async-start | bytes 73728
  907.0 198.4 %reduce-scatter.58.cloned.1.call-start = ((), (), s32[]{:S(2)}) async-start(), calls=%async_computation.31 | async-start | bytes 73728
  907.9 228.6 %reduce-scatter.60.cloned.1.call-start = ((), (), s32[]{:S(2)}) async-start(), calls=%async_computation.32 | async-start | bytes 73728
  908.7 258.8 %reduce-scatter.46.cloned.1.call-start = ((), (), s32[]{:S(2)}) async-start(), calls=%async_computation.25 | async-start | bytes 442368 | tf_op jit(solution)/shard_map/reduce_scatter | solution.py:425
  910.8 287.8 %reduce-scatter.48.cloned.1.call-start = ((), (), s32[]{:S(2)}) async-start(), calls=%async_computation.26 | async-start | bytes 442368 | tf_op jit(solution)/shard_map/reduce_scatter | solution.py:428
  918.1 313.5 %reduce-scatter.42.cloned.1.call-start = ((), (), s32[]{:S(2)}) async-start(), calls=%async_computation.23 | async-start | bytes 1327104 | tf_op jit(solution)/shard_map/reduce_scatter | solution.py:398
  927.0 360.0 %reduce-scatter.72.cloned.1.call-start = ((), (), s32[]{:S(2)}) async-start(), calls=%async_computation.38 | async-start | bytes 5308416
  943.8 376.3 %reduce-scatter.54.cloned.1.call-start = ((), (), s32[]{:S(2)}) async-start(), calls=%async_computation.29 | async-start | bytes 1327104 | tf_op jit(solution)/shard_map/reduce_scatter | solution.py:449
  948.2 405.4 %reduce-scatter.50.cloned.1.call-start = ((), (), s32[]{:S(2)}) async-start(), calls=%async_computation.27 | async-start | bytes 1327104 | tf_op jit(solution)/shard_map/reduce_scatter | solution.py:431
  953.1 433.8 %reduce-scatter.44.cloned.1.call-start = ((), (), s32[]{:S(2)}) async-start(), calls=%async_computation.24 | async-start | bytes 1327104 | tf_op jit(solution)/shard_map/reduce_scatter | solution.py:422
  957.5 473.5 %reduce-scatter.52.cloned.1.call-start = ((), (), s32[]{:S(2)}) async-start(), calls=%async_computation.28 | async-start | bytes 3981312 | tf_op jit(solution)/shard_map/reduce_scatter | solution.py:446
  967.1 519.9 %reduce-scatter.56.cloned.1.call-start = ((), (), s32[]{:S(2)}) async-start(), calls=%async_computation.30 | async-start | bytes 5308416 | tf_op jit(solution)/shard_map/reduce_scatter | solution.py:470
  978.6 556.5 %all-reduce.7.cloned.1.call-start = ((), (), s32[]{:S(2)}) async-start(), calls=%async_computation.40 | async-start | bytes 205824 | tf_op jit(solution)/shard_map/psum | solution.py:477
  1047.1 90.7 %collective-permute-start.2 = (bf16[4,1,64,256]{3,2,1,0:T(8,128)(2,1)}, bf16[4,1,64,256]{3,2,1,0:T(8,128)(2,1)}, u32[]{:S(2)}, u32[]{:S(2)}) collective-permute-start(bf16[4,1,64,256]{3,2,1,0:T(8,128)(2,1)} %get-tuple-element.811), channel_id=1, source_target_pairs={{0,1},{1,2},{2,3},{3,4},{4,5},{5,6},{6,7},{8,9},{9,10},{10,11},{11... | collective-permute-start | bytes 393224 | tf_op jit(solution)/shard_map/ppermute | solution.py:33
  1049.0 88.7 %collective-permute-start.3 = (bf16[4,1,64,256]{3,2,1,0:T(8,128)(2,1)}, bf16[4,1,64,256]{3,2,1,0:T(8,128)(2,1)}, u32[]{:S(2)}, u32[]{:S(2)}) collective-permute-start(bf16[4,1,64,256]{3,2,1,0:T(8,128)(2,1)} %get-tuple-element.812), channel_id=1, source_target_pairs={{1,0},{2,1},{3,2},{4,3},{5,4},{6,5},{7,6},{9,8},{10,9},{11,10},{12... | collective-permute-start | bytes 393224 | tf_op jit(solution)/shard_map/ppermute | solution.py:35
  1198.6 417.3 %all-reduce.9.cloned.1.call-start = ((), (), s32[]{:S(2)}) async-start(), calls=%async_computation.41 | async-start | bytes 4653056 | tf_op jit(solution)/shard_map/psum | solution.py:476
  (133 other events, 477.7 us)
Sparse Core Ops, SparseCore 0:
  36.9 28.5 all-gather.2
  67.7 24.5 all-gather.4
  818.0 33.8 reduce-scatter.37
  854.0 32.2 reduce-scatter.39
  889.1 28.2 reduce-scatter.69
  920.1 28.3 reduce-scatter.67
  951.4 28.4 reduce-scatter.65
  982.7 28.4 reduce-scatter.63
  1014.1 29.6 reduce-scatter.73
  1046.0 28.4 reduce-scatter.61
  1077.3 28.1 reduce-scatter.57
  1108.2 28.1 reduce-scatter.59
  1138.7 28.7 reduce-scatter.45
  1169.7 28.8 reduce-scatter.47
  1200.7 30.9 reduce-scatter.41
  1233.8 53.1 reduce-scatter.71
  1289.2 30.9 reduce-scatter.53
  1322.3 31.2 reduce-scatter.49
  1355.9 30.9 reduce-scatter.43
  1389.0 41.9 reduce-scatter.51
  1433.4 53.4 reduce-scatter.55
  1493.1 41.9 all-reduce.6
  1539.6 76.1 all-reduce.8
where the time goes:
time: 1640 us; the launch traced here: 1630 us
  waiting for transfers between devices  638 us (39%)
  matrix products  487 us (30%)
  local copies, waits for them, and re-layouts  250 us (15%)
  other arithmetic  216 us (13%)
  loops' own time  17.9 us (1%)
    unnamed x32, waiting for transfers between devices  161 us
    dot_general x18, matrix products, fast_dot(): return jnp.dot(left, right, preferred_element_type=jnp.float32)  127 us
    convert_element_type x4, other arithmetic, one_block(): score_grad = (softmax_probs * (prob_grad - row_dot)).astype(jnp.bfloat16)  88.8 us
    dot_general x8, matrix products, block_scores(): jnp.einsum('qhd,khd->hqk', split_heads(query_block), split_heads(key_rows...  83.7 us
    unnamed x219, local copies, waits for them, and re-layouts  79.8 us
    dot_general x4, matrix products, one_block(): jnp.einsum('qhd,khd->hqk', grad_heads, split_heads(value_rows), preferred...  75.3 us
    psum x1, waiting for transfers between devices, on_device(): lax.psum(shares[0].astype(jnp.bfloat16), 'dp').astype(jnp.float32)  68.6 us
    reduce_scatter x1, waiting for transfers between devices, on_device(): lax.psum_scatter(down_weight_grad.astype(jnp.bfloat16), 'row', scatter_di...  55.9 us
  transfers between devices with their start and end apart: 27, of which 20 were waited for; matrix products, arithmetic and copies ran while one was open for 13% of the time, Pallas kernels for 0%

commit v1 on v0

v1 whole, which is shorter than its diff:
```python
import functools
import math
import jax
import jax.numpy as jnp
from jax import lax
from jax.experimental import pallas as pl
from jax.experimental.pallas import tpu as pltpu
from jax.sharding import PartitionSpec as P

D = 768
HD = 64
PAIR = 128
BLOCK = 256
KEYS = 256
CLIPS = 4
FAR = 2.0**100
SCALE = 0.125
f32 = jnp.float32
bf16 = jnp.bfloat16
VMEM_ASK = 48 * 2**20


def lane_of(rows):
    return lax.broadcasted_iota(jnp.int32, (rows, PAIR), 1)


def dot_nt(left, right):
    return lax.dot_general(left, right, (((1,), (1,)), ((), ())), preferred_element_type=f32)


def dot_nn(left, right):
    return lax.dot_general(left, right, (((1,), (0,)), ((), ())), preferred_element_type=f32)


def three_terms(value):
    high = value.astype(bf16).astype(f32)
    rest = value - high
    middle = rest.astype(bf16).astype(f32)
    return high, middle, rest - middle


def tagged(extra, value, half):
    high, middle, low = three_terms(value)
    extra = jnp.where(half == 8, -high, extra)
    extra = jnp.where(half == 9, -middle, extra)
    return jnp.where(half == 10, -low, extra)


def segment_tags(segment_row):
    lane = jnp.arange(PAIR, dtype=jnp.int32) % HD
    wrong = (lane[None, :] < CLIPS) & (lane[None, :] != segment_row[:, None])
    return jnp.where(wrong, -FAR, 0.0).astype(bf16)


def key_tags(segment_row):
    lane = jnp.arange(PAIR, dtype=jnp.int32) % HD
    ones = (lane[None, :] == segment_row[:, None]) | ((lane[None, :] >= 8) & (lane[None, :] <= 10))
    return jnp.where(ones, 1.0, 0.0).astype(bf16)


def clip_key_tags(rows, clip):
    half = lane_of(rows) % HD
    return jnp.where((half == clip) | ((half >= 8) & (half <= 10)), 1.0, 0.0).astype(bf16)


def cross_forward_kernel(
    seg_ref, frame_ref, q_ref, pooled_ref, key_w_ref, value_w_ref, tag_ref, col_ref,
    out_ref, extra_ref, keys_s, values_s,
):
    keys_s[...] = dot_nn(pooled_ref[...], key_w_ref[...]).astype(bf16)
    values_s[...] = dot_nn(pooled_ref[...], value_w_ref[...]).astype(bf16)
    left = lane_of(BLOCK) < HD
    half = lane_of(BLOCK) % HD
    for block in range(q_ref.shape[0] // BLOCK):
        rows = pl.ds(block * BLOCK, BLOCK)
        query = (q_ref[rows, :].astype(f32) * SCALE).astype(bf16)
        tags = tag_ref[rows, :]
        query_a = jnp.where(left, query, tags)
        query_b = jnp.where(left, tags, query)

        def one_clip(clip, carry, rows=rows, query_a=query_a, query_b=query_b, tags=tags):
            own = pl.ds(pl.multiple_of(frame_ref[clip] * KEYS, KEYS), KEYS)
            key = keys_s[own, :]
            value = values_s[own, :]
            key_tag = clip_key_tags(KEYS, clip)
            one = jnp.ones_like(value)
            score_a = dot_nt(query_a, jnp.where(left, key, key_tag))
            score_b = dot_nt(query_b, jnp.where(left, key_tag, key))
            top_a = jnp.max(score_a, -1, keepdims=True)
            top_b = jnp.max(score_b, -1, keepdims=True)
            exp_a = jnp.exp(score_a - top_a).astype(bf16)
            exp_b = jnp.exp(score_b - top_b).astype(bf16)
            mix_a = dot_nn(exp_a, jnp.where(left, value, one))
            mix_b = dot_nn(exp_b, jnp.where(left, one, value))
            total = jnp.where(left, mix_b, mix_a)
            mixed = jnp.where(left, mix_a, mix_b) / pltpu.roll(total, HD, 1)
            log_sum = jnp.where(left, top_b, top_a) + jnp.log(total)
            extra = tagged(tags.astype(f32), log_sum, half)
            mine = col_ref[rows, :] == clip
            out_ref[rows, :] = jnp.where(mine, mixed, out_ref[rows, :].astype(f32)).astype(bf16)
            extra_ref[rows, :] = jnp.where(mine, extra, extra_ref[rows, :].astype(f32)).astype(bf16)
            return carry

        lax.fori_loop(seg_ref[block * BLOCK], seg_ref[block * BLOCK + BLOCK - 1] + 1, one_clip, 0)


def pair_spec(rows):
    return pl.BlockSpec((rows, PAIR), lambda p, *_: (0, p))


def whole_spec(shape):
    return pl.BlockSpec(shape, lambda p, *_: (0,) * len(shape))


def cross_forward(segments, frames, queries, pooled, key_w, value_w, tags):
    rows = queries.shape[0]
    return pl.pallas_call(
        cross_forward_kernel,
        out_shape=(
            jax.ShapeDtypeStruct((rows, D), bf16),
            jax.ShapeDtypeStruct((rows, D), bf16),
        ),
        grid_spec=pltpu.PrefetchScalarGridSpec(
            num_scalar_prefetch=2,
            grid=(D // PAIR,),
            in_specs=[
                pair_spec(rows),
                whole_spec(pooled.shape),
                pair_spec(key_w.shape[0]),
                pair_spec(key_w.shape[0]),
                whole_spec((rows, PAIR)),
                whole_spec((rows, 1)),
            ],
            out_specs=[pair_spec(rows), pair_spec(rows)],
            scratch_shapes=[
                pltpu.VMEM((pooled.shape[0], PAIR), bf16),
                pltpu.VMEM((pooled.shape[0], PAIR), bf16),
            ],
        ),
        compiler_params=pltpu.CompilerParams(vmem_limit_bytes=VMEM_ASK),
        cost_estimate=pl.CostEstimate(
            flops=12_000_000_000, bytes_accessed=8_000_000, transcendentals=4_000_000
        ),
        name="cross_forward",
    )(segments, frames, queries, pooled, key_w, value_w, tags, segments[:, None])


def self_forward_kernel(
    first_ref, q_ref, k_ref, v_ref, tag_ref, key_tag_ref,
    out_ref, extra_ref, mix_a_s, mix_b_s, top_s,
):
    left = lane_of(BLOCK) < HD
    half = lane_of(BLOCK) % HD
    row_at = lax.broadcasted_iota(jnp.int32, (BLOCK, BLOCK), 0)
    col_at = lax.broadcasted_iota(jnp.int32, (BLOCK, BLOCK), 1)
    for block in range(q_ref.shape[0] // BLOCK):
        rows = pl.ds(block * BLOCK, BLOCK)
        query = (q_ref[rows, :].astype(f32) * SCALE).astype(bf16)
        tags = tag_ref[rows, :]
        query_a = jnp.where(left, query, tags)
        query_b = jnp.where(left, tags, query)

        def scores(own, query_a=query_a, query_b=query_b):
            key = k_ref[own, :]
            value = v_ref[own, :]
            key_tag = key_tag_ref[own, :]
            one = jnp.ones_like(value)
            score_a = dot_nt(query_a, jnp.where(left, key, key_tag))
            score_b = dot_nt(query_b, jnp.where(left, key_tag, key))
            return score_a, score_b, jnp.where(left, value, one), jnp.where(left, one, value)

        score_a, score_b, value_a, value_b = scores(rows)
        score_a = jnp.where(row_at >= col_at, score_a, -FAR)
        score_b = jnp.where(row_at >= col_at, score_b, -FAR)
        top_a = jnp.max(score_a, -1, keepdims=True)
        top_b = jnp.max(score_b, -1, keepdims=True)
        mix_a_s[...] = dot_nn(jnp.exp(score_a - top_a).astype(bf16), value_a)
        mix_b_s[...] = dot_nn(jnp.exp(score_b - top_b).astype(bf16), value_b)
        top_s[...] = jnp.where(left, top_a, top_b)

        if block:

            def one_block(other, carry, scores=scores):
                own = pl.ds(pl.multiple_of(other * BLOCK, BLOCK), BLOCK)
                score_a, score_b, value_a, value_b = scores(own)
                old_a = top_s[:, 0:1]
                old_b = top_s[:, HD : HD + 1]
                top_a = jnp.maximum(old_a, jnp.max(score_a, -1, keepdims=True))
                top_b = jnp.maximum(old_b, jnp.max(score_b, -1, keepdims=True))
                mix_a_s[...] = mix_a_s[...] * jnp.exp(old_a - top_a) + dot_nn(
                    jnp.exp(score_a - top_a).astype(bf16), value_a
                )
                mix_b_s[...] = mix_b_s[...] * jnp.exp(old_b - top_b) + dot_nn(
                    jnp.exp(score_b - top_b).astype(bf16), value_b
                )
                top_s[...] = jnp.where(left, top_a, top_b)
                return carry

            lax.fori_loop(first_ref[block], block, one_block, 0)

        total = jnp.where(left, mix_b_s[...], mix_a_s[...])
        mixed = jnp.where(left, mix_a_s[...], mix_b_s[...]) / pltpu.roll(total, HD, 1)
        log_sum = pltpu.roll(top_s[...], HD, 1) + jnp.log(total)
        out_ref[rows, :] = mixed.astype(bf16)
        extra_ref[rows, :] = tagged(tags.astype(f32), log_sum, half).astype(bf16)


def self_forward(first_blocks, packed, tags, key_tag):
    rows = packed.shape[0]
    pairs = D // PAIR
    shifted = lambda by: pl.BlockSpec((rows, PAIR), lambda p, *_: (0, p + by))
    return pl.pallas_call(
        self_forward_kernel,
        out_shape=(
            jax.ShapeDtypeStruct((rows, D), bf16),
            jax.ShapeDtypeStruct((rows, D), bf16),
        ),
        grid_spec=pltpu.PrefetchScalarGridSpec(
            num_scalar_prefetch=1,
            grid=(pairs,),
            in_specs=[
                shifted(0), shifted(pairs), shifted(2 * pairs),
                whole_spec((rows, PAIR)), whole_spec((rows, PAIR)),
            ],
            out_specs=[pair_spec(rows), pair_spec(rows)],
            scratch_shapes=[pltpu.VMEM((BLOCK, PAIR), f32)] * 3,
        ),
        compiler_params=pltpu.CompilerParams(vmem_limit_bytes=VMEM_ASK),
        cost_estimate=pl.CostEstimate(
            flops=12_000_000_000, bytes_accessed=8_000_000, transcendentals=4_000_000
        ),
        name="self_forward",
    )(first_blocks, packed, packed, packed, tags, key_tag)


def grad_rows(mixed, grad, left, half):
    product = mixed.astype(f32) * grad.astype(f32)
    dot_a = jnp.sum(jnp.where(left, product, 0.0), -1, keepdims=True)
    dot_b = jnp.sum(jnp.where(left, 0.0, product), -1, keepdims=True)
    extra = tagged(jnp.zeros_like(product), jnp.where(left, dot_b, dot_a), half).astype(bf16)
    return jnp.where(left, grad, extra), jnp.where(left, extra, grad)


def back_products(query_a, query_b, grad_a, grad_b, key, value, key_tag, left, masked=None):
    key_a = jnp.where(left, key, key_tag)
    key_b = jnp.where(left, key_tag, key)
    score_a = dot_nt(query_a, key_a)
    score_b = dot_nt(query_b, key_b)
    if masked is not None:
        score_a = jnp.where(masked, score_a, -FAR)
        score_b = jnp.where(masked, score_b, -FAR)
    prob_a = jnp.exp(score_a)
    prob_b = jnp.exp(score_b)
    back_a = (prob_a * dot_nt(grad_a, jnp.where(left, value, key_tag))).astype(bf16)
    back_b = (prob_b * dot_nt(grad_b, jnp.where(left, key_tag, value))).astype(bf16)
    query_grad = jnp.where(left, dot_nn(back_a, key_a), dot_nn(back_b, key_b))
    return prob_a.astype(bf16), prob_b.astype(bf16), back_a, back_b, query_grad


def cross_backward_kernel(
    seg_ref, frame_ref, q_ref, pooled_ref, key_w_ref, value_w_ref, extra_ref, mixed_ref, grad_ref,
    dq_ref, dk_ref, dv_ref, keys_s, values_s, dk_s, dv_s, dq_s,
):
    keys_s[...] = dot_nn(pooled_ref[...], key_w_ref[...]).astype(bf16)
    values_s[...] = dot_nn(pooled_ref[...], value_w_ref[...]).astype(bf16)
    dk_s[...] = jnp.zeros_like(dk_s)
    dv_s[...] = jnp.zeros_like(dv_s)
    left = lane_of(BLOCK) < HD
    half = lane_of(BLOCK) % HD
    for block in range(q_ref.shape[0] // BLOCK):
        rows = pl.ds(block * BLOCK, BLOCK)
        query = (q_ref[rows, :].astype(f32) * SCALE).astype(bf16)
        extra = extra_ref[rows, :]
        grad = grad_ref[rows, :]
        query_a = jnp.where(left, query, extra)
        query_b = jnp.where(left, extra, query)
        grad_a, grad_b = grad_rows(mixed_ref[rows, :], grad, left, half)
        query_t = query.T
        grad_t = grad.T
        dq_s[...] = jnp.zeros_like(dq_s)

        def one_clip(clip, carry, query_a=query_a, query_b=query_b, grad_a=grad_a, grad_b=grad_b,
                     query_t=query_t, grad_t=grad_t):
            own = pl.ds(pl.multiple_of(frame_ref[clip] * KEYS, KEYS), KEYS)
            prob_a, prob_b, back_a, back_b, query_grad = back_products(
                query_a, query_b, grad_a, grad_b, keys_s[own, :], values_s[own, :],
                clip_key_tags(KEYS, clip), left,
            )
            dq_s[...] += query_grad
            dk_s[0:HD, own] += dot_nn(query_t[0:HD], back_a)
            dk_s[HD:PAIR, own] += dot_nn(query_t[HD:PAIR], back_b)
            dv_s[0:HD, own] += dot_nn(grad_t[0:HD], prob_a)
            dv_s[HD:PAIR, own] += dot_nn(grad_t[HD:PAIR], prob_b)
            return carry

        lax.fori_loop(seg_ref[block * BLOCK], seg_ref[block * BLOCK + BLOCK - 1] + 1, one_clip, 0)
        dq_ref[rows, :] = (dq_s[...] * SCALE).astype(bf16)
    dk_ref[...] = dk_s[...].astype(bf16)
    dv_ref[...] = dv_s[...].astype(bf16)


def cross_backward(segments, frames, queries, pooled, key_w, value_w, extra, mixed, grad):
    rows = queries.shape[0]
    keys = pooled.shape[0]
    upright = pl.BlockSpec((PAIR, keys), lambda p, *_: (p, 0))
    return pl.pallas_call(
        cross_backward_kernel,
        out_shape=(
            jax.ShapeDtypeStruct((rows, D), bf16),
            jax.ShapeDtypeStruct((D, keys), bf16),
            jax.ShapeDtypeStruct((D, keys), bf16),
        ),
        grid_spec=pltpu.PrefetchScalarGridSpec(
            num_scalar_prefetch=2,
            grid=(D // PAIR,),
            in_specs=[
                pair_spec(rows),
                whole_spec(pooled.shape),
                pair_spec(key_w.shape[0]),
                pair_spec(key_w.shape[0]),
                pair_spec(rows), pair_spec(rows), pair_spec(rows),
            ],
            out_specs=[pair_spec(rows), upright, upright],
            scratch_shapes=[
                pltpu.VMEM((keys, PAIR), bf16),
                pltpu.VMEM((keys, PAIR), bf16),
                pltpu.VMEM((PAIR, keys), f32),
                pltpu.VMEM((PAIR, keys), f32),
                pltpu.VMEM((BLOCK, PAIR), f32),
            ],
        ),
        compiler_params=pltpu.CompilerParams(vmem_limit_bytes=VMEM_ASK),
        cost_estimate=pl.CostEstimate(
            flops=24_000_000_000, bytes_accessed=16_000_000, transcendentals=4_000_000
        ),
        name="cross_backward",
    )(segments, frames, queries, pooled, key_w, value_w, extra, mixed, grad)


def self_backward_kernel(
    first_ref, q_ref, k_ref, v_ref, key_tag_ref, extra_ref, mixed_ref, grad_ref,
    dq_ref, dk_ref, dv_ref, dk_s, dv_s, dq_s,
):
    dk_s[...] = jnp.zeros_like(dk_s)
    dv_s[...] = jnp.zeros_like(dv_s)
    left = lane_of(BLOCK) < HD
    half = lane_of(BLOCK) % HD
    row_at = lax.broadcasted_iota(jnp.int32, (BLOCK, BLOCK), 0)
    col_at = lax.broadcasted_iota(jnp.int32, (BLOCK, BLOCK), 1)
    for block in range(q_ref.shape[0] // BLOCK):
        rows = pl.ds(block * BLOCK, BLOCK)
        query = (q_ref[rows, :].astype(f32) * SCALE).astype(bf16)
        extra = extra_ref[rows, :]
        grad = grad_ref[rows, :]
        query_a = jnp.where(left, query, extra)
        query_b = jnp.where(left, extra, query)
        grad_a, grad_b = grad_rows(mixed_ref[rows, :], grad, left, half)
        query_t = query.T
        grad_t = grad.T

        def one_block(own, masked=None, query_a=query_a, query_b=query_b, grad_a=grad_a,
                      grad_b=grad_b, query_t=query_t, grad_t=grad_t):
            prob_a, prob_b, back_a, back_b, query_grad = back_products(
                query_a, query_b, grad_a, grad_b, k_ref[own, :], v_ref[own, :],
                key_tag_ref[own, :], left, masked,
            )
            dk_s[0:HD, own] += dot_nn(query_t[0:HD], back_a)
            dk_s[HD:PAIR, own] += dot_nn(query_t[HD:PAIR], back_b)
            dv_s[0:HD, own] += dot_nn(grad_t[0:HD], prob_a)
            dv_s[HD:PAIR, own] += dot_nn(grad_t[HD:PAIR], prob_b)
            return query_grad

        dq_s[...] = one_block(rows, row_at >= col_at)
        if block:

            def step(other, carry, one_block=one_block):
                dq_s[...] += one_block(pl.ds(pl.multiple_of(other * BLOCK, BLOCK), BLOCK))
                return carry

            lax.fori_loop(first_ref[block], block, step, 0)
        dq_ref[rows, :] = (dq_s[...] * SCALE).astype(bf16)
    dk_ref[...] = dk_s[...].T.astype(bf16)
    dv_ref[...] = dv_s[...].T.astype(bf16)


def self_backward(first_blocks, packed, key_tag, extra, mixed, grad):
    rows = packed.shape[0]
    pairs = D // PAIR
    shifted = lambda by: pl.BlockSpec((rows, PAIR), lambda p, *_: (0, p + by))
    return pl.pallas_call(
        self_backward_kernel,
        out_shape=(jax.ShapeDtypeStruct((rows, D), bf16),) * 3,
        grid_spec=pltpu.PrefetchScalarGridSpec(
            num_scalar_prefetch=1,
            grid=(pairs,),
            in_specs=[
                shifted(0), shifted(pairs), shifted(2 * pairs), whole_spec((rows, PAIR)),
                pair_spec(rows), pair_spec(rows), pair_spec(rows),
            ],
            out_specs=[pair_spec(rows)] * 3,
            scratch_shapes=[
                pltpu.VMEM((PAIR, rows), f32),
                pltpu.VMEM((PAIR, rows), f32),
                pltpu.VMEM((BLOCK, PAIR), f32),
            ],
        ),
        compiler_params=pltpu.CompilerParams(vmem_limit_bytes=VMEM_ASK),
        cost_estimate=pl.CostEstimate(
            flops=24_000_000_000, bytes_accessed=16_000_000, transcendentals=4_000_000
        ),
        name="self_backward",
    )(first_blocks, packed, packed, packed, key_tag, extra, mixed, grad)


def first_block_table(segment_row):
    clips = jnp.arange(CLIPS, dtype=jnp.int32)
    starts = jnp.sum((segment_row[:, None] < clips[None, :]).astype(jnp.int32), 0)
    heads = segment_row[::BLOCK]
    first = jnp.sum(jnp.where(heads[:, None] == clips[None, :], starts[None, :], 0), 1)
    return (first // BLOCK).astype(jnp.int32)


epsilon = 1e-05
ROOT = math.sqrt(2.0 / math.pi)
CUBE = 0.044715
C = 256
IMG = 64
POOL = 4


TILE = 256


def dot_tn(left, right):
    return lax.dot_general(left, right, (((0,), (0,)), ((), ())), preferred_element_type=f32)


def normalized(values):
    average = jnp.mean(values, -1, keepdims=True)
    centred = values - average
    spread = lax.rsqrt(jnp.mean(centred * centred, -1, keepdims=True) + epsilon)
    return centred * spread, spread


def norm_back(unit, spread, gain, grad):
    scaled = grad * gain
    mean_scaled = jnp.mean(scaled, -1, keepdims=True)
    mean_along = jnp.mean(scaled * unit, -1, keepdims=True)
    lead = tuple(range(grad.ndim - 1))
    return (
        (scaled - mean_scaled - unit * mean_along) * spread,
        jnp.sum(grad * unit, lead),
        jnp.sum(grad, lead),
    )


def gelu_and_slope(value):
    square = value * value
    bent = jnp.tanh(value * (ROOT + (ROOT * CUBE) * square))
    half = 0.5 + 0.5 * bent
    slope = half + value * (0.5 - 0.5 * bent * bent) * (ROOT + (3.0 * ROOT * CUBE) * square)
    return value * half, slope


def tiles_of(count):
    return [pl.ds(at, TILE) for at in range(0, count, TILE)]


def feed_forward_kernel(
    middle_ref, mixed_ref, join_ref, gain_ref, shift_ref, up_ref, bias_ref, down_ref, grad_ref,
    out_ref, second_ref, low_ref, mixed_grad_ref, join_grad_ref, gain_grad_ref, shift_grad_ref,
    bias_grad_ref, chunk_ref,
    normed_s, grad_t_s, back_s, hidden_s, pre_grad_s, up_s, down_s, sems,
):
    step = pl.program_id(0)
    steps = pl.num_programs(0)
    rows = middle_ref.shape[0]
    shares, deep = chunk_ref.shape[0], chunk_ref.shape[1] // 2
    group, narrow = D // deep, D // shares

    @pl.when(step == 0)
    def _():
        for at in tiles_of(rows):
            total = middle_ref[at, :] + dot_nn(mixed_ref[at, :], join_ref[...])
            out_ref[at, :] = total
            second_ref[at, :] = total
            unit, _ = normalized(total)
            normed_s[at, :] = (unit * gain_ref[...] + shift_ref[...]).astype(bf16)
            back_s[at, :] = jnp.zeros((TILE, D), f32)
            grad_t_s[:, at] = grad_ref[at, :].T

    bias_grad = jnp.zeros((1, D), f32)
    for at in tiles_of(rows):
        hidden, slope = gelu_and_slope(dot_nn(normed_s[at, :], up_ref[...]) + bias_ref[...])
        hidden = hidden.astype(bf16)
        hidden_s[at, :] = hidden
        pre_grad = (dot_nt(grad_ref[at, :], down_ref[...]) * slope).astype(bf16)
        pre_grad_s[at, :] = pre_grad
        bias_grad += jnp.sum(pre_grad.astype(f32), 0, keepdims=True)
        out_ref[at, :] += dot_nn(hidden, down_ref[...])
        back_s[at, :] += dot_nt(pre_grad, up_ref[...])
    bias_grad_ref[...] = bias_grad
    up_s[step] = dot_tn(pre_grad_s[...], normed_s[...]).astype(bf16).reshape(group, deep, D)
    down_s[step] = dot_nn(grad_t_s[...], hidden_s[...]).astype(bf16).reshape(shares, narrow, D)

    def copies(at):
        return (
            pltpu.make_async_copy(
                up_s.at[at], chunk_ref.at[pl.ds(at * group, group), pl.ds(0, deep)], sems.at[0, at]
            ),
            pltpu.make_async_copy(
                down_s.at[at],
                chunk_ref.at[:, pl.ds(pl.multiple_of(deep + at * narrow, 16), narrow)],
                sems.at[1, at],
            ),
        )

    for copy in copies(step):
        copy.start()

    @pl.when(step == steps - 1)
    def _():
        gain_grad = jnp.zeros((1, D), f32)
        shift_grad = jnp.zeros((1, D), f32)
        for at in tiles_of(rows):
            unit, spread = normalized(second_ref[at, :])
            part, one, two = norm_back(unit, spread, gain_ref[...], back_s[at, :])
            gain_grad += one[None]
            shift_grad += two[None]
            total = grad_ref[at, :].astype(f32) + part
            second_ref[at, :] = total
            low = total.astype(bf16)
            low_ref[at, :] = low
            mixed_grad_ref[at, :] = dot_nt(low, join_ref[...]).astype(bf16)
        gain_grad_ref[...] = gain_grad
        shift_grad_ref[...] = shift_grad
        join_grad_ref[...] = dot_tn(low_ref[...], mixed_ref[...]).astype(bf16)
        for at in range(FF // D):
            for copy in copies(at):
                copy.wait()


FF = 3072


def still(shape):
    return pl.BlockSpec(shape, lambda *_: (0,) * len(shape), pipeline_mode=pl.Buffered(1))


def feed_forward(middle, mixed, join, gain, shift, up, bias, down, grad, shares):
    rows = middle.shape[0]
    steps = FF // D
    deep = FF // shares
    tall = still((rows, D))
    row = still((1, D))
    return pl.pallas_call(
        feed_forward_kernel,
        out_shape=(
            jax.ShapeDtypeStruct((rows, D), f32),
            jax.ShapeDtypeStruct((rows, D), f32),
            jax.ShapeDtypeStruct((rows, D), bf16),
            jax.ShapeDtypeStruct((rows, D), bf16),
            jax.ShapeDtypeStruct((D, D), bf16),
            jax.ShapeDtypeStruct((1, D), f32),
            jax.ShapeDtypeStruct((1, D), f32),
            jax.ShapeDtypeStruct((1, FF), f32),
            jax.ShapeDtypeStruct((shares, 2 * deep, D), bf16),
        ),
        grid_spec=pltpu.PrefetchScalarGridSpec(
            num_scalar_prefetch=0,
            grid=(steps,),
            in_specs=[
                tall, tall, still((D, D)), row, row,
                pl.BlockSpec((D, D), lambda j: (0, j)),
                pl.BlockSpec((1, D), lambda j: (0, j)),
                pl.BlockSpec((D, D), lambda j: (j, 0)),
                tall,
            ],
            out_specs=[
                tall, tall, tall, tall, still((D, D)), row, row,
                pl.BlockSpec((1, D), lambda j: (0, j)),
                pl.BlockSpec(memory_space=pl.ANY),
            ],
            scratch_shapes=[
                pltpu.VMEM((rows, D), bf16),
                pltpu.VMEM((D, rows), bf16),
                pltpu.VMEM((rows, D), f32),
                pltpu.VMEM((rows, D), bf16),
                pltpu.VMEM((rows, D), bf16),
                pltpu.VMEM((steps, D // deep, deep, D), bf16),
                pltpu.VMEM((steps, shares, D // shares, D), bf16),
                pltpu.SemaphoreType.DMA((2, steps)),
            ],
        ),
        compiler_params=pltpu.CompilerParams(vmem_limit_bytes=56 * 2**20),
        cost_estimate=pl.CostEstimate(
            flops=34_000_000_000, bytes_accessed=40_000_000, transcendentals=3_200_000
        ),
        name="feed_forward",
    )(middle, mixed, join, gain[None], shift[None], up, bias[None], down, grad)


def project_back_kernel(
    query_ref, key_ref, value_ref, project_ref, middle_ref, second_ref, gain_ref, shift_ref,
    join_ref, mixed_ref,
    middle_grad_ref, mixed_grad_ref, project_grad_ref, join_grad_ref, gain_grad_ref, shift_grad_ref,
    normed_s, low_s,
):
    rows = middle_ref.shape[0]
    gain_grad = jnp.zeros((1, D), f32)
    shift_grad = jnp.zeros((1, D), f32)
    for at in tiles_of(rows):
        back = dot_nt(query_ref[at, :], project_ref[:, 0:D])
        back += dot_nt(key_ref[at, :], project_ref[:, D : 2 * D])
        back += dot_nt(value_ref[at, :], project_ref[:, 2 * D : 3 * D])
        unit, spread = normalized(middle_ref[at, :])
        normed_s[at, :] = (unit * gain_ref[...] + shift_ref[...]).astype(bf16)
        part, one, two = norm_back(unit, spread, gain_ref[...], back)
        gain_grad += one[None]
        shift_grad += two[None]
        total = second_ref[at, :] + part
        middle_grad_ref[at, :] = total
        low = total.astype(bf16)
        low_s[at, :] = low
        mixed_grad_ref[at, :] = dot_nt(low, join_ref[...]).astype(bf16)
    gain_grad_ref[...] = gain_grad
    shift_grad_ref[...] = shift_grad
    project_grad_ref[0:D] = dot_tn(query_ref[...], normed_s[...]).astype(bf16)
    project_grad_ref[D : 2 * D] = dot_tn(key_ref[...], normed_s[...]).astype(bf16)
    project_grad_ref[2 * D : 3 * D] = dot_tn(value_ref[...], normed_s[...]).astype(bf16)
    join_grad_ref[...] = dot_tn(low_s[...], mixed_ref[...]).astype(bf16)


def project_back(query, key, value, project, middle, second, gain, shift, join, mixed):
    rows = middle.shape[0]
    return pl.pallas_call(
        project_back_kernel,
        out_shape=(
            jax.ShapeDtypeStruct((rows, D), f32),
            jax.ShapeDtypeStruct((rows, D), bf16),
            jax.ShapeDtypeStruct((3 * D, D), bf16),
            jax.ShapeDtypeStruct((D, D), bf16),
            jax.ShapeDtypeStruct((1, D), f32),
            jax.ShapeDtypeStruct((1, D), f32),
        ),
        in_specs=[pl.BlockSpec(memory_space=pltpu.VMEM)] * 10,
        out_specs=[pl.BlockSpec(memory_space=pltpu.VMEM)] * 6,
        scratch_shapes=[pltpu.VMEM((rows, D), bf16), pltpu.VMEM((rows, D), bf16)],
        compiler_params=pltpu.CompilerParams(vmem_limit_bytes=56 * 2**20),
        cost_estimate=pl.CostEstimate(
            flops=10_000_000_000, bytes_accessed=30_000_000, transcendentals=2_000
        ),
        name="project_back",
    )(query, key, value, project, middle, second, gain[None], shift[None], join, mixed)


MESH = pl.DeviceIdType.MESH


def bits_of(count):
    return count.bit_length() - 1


def plan_streams(rows, dp, orders):
    unit = 16 * dp
    units = rows // unit
    sizes = [units // len(orders) + (i < units % len(orders)) for i in range(len(orders))]
    plan, at = [], 0
    for order, size in zip(orders, sizes):
        if size:
            plan.append((at * unit, size * unit, order))
            at += size
    return plan


def stream_steps(count, kind_order, dp_bits, q_bits):
    dp_up = [("dp", b) for b in range(dp_bits)]
    dp_down = dp_up[::-1]
    q_steps = [("q", b) for b in range(q_bits)]
    return {
        "up": dp_up + q_steps,
        "down": dp_down + q_steps,
        "q_up": q_steps + dp_up,
        "q_down": q_steps + dp_down,
    }[kind_order]


def reduce_kernel(layout, dp, row, *refs):
    (partial_ref, summed_ref, out_ref), refs = refs[:3], refs[3:]
    accs, refs = refs[: len(layout)], refs[len(layout) :]
    n_recv = sum(len(item[3]) + (item[0] == 0) for item in layout)
    recvs, (send_sem, recv_sem, local_sem) = refs[:n_recv], refs[n_recv:]
    me_dp, me_row = lax.axis_index("dp"), lax.axis_index("row")
    core = lax.rem(me_row, 2)
    me_q = me_row // 2
    q_bits = bits_of(row // 2)

    def bit(value, b):
        return lax.rem(value // (2**b), 2)

    def partner(step):
        kind, b = step
        if kind == "core":
            return me_dp, me_row + 1 - 2 * core
        if kind == "dp":
            return me_dp + (2**b) * (1 - 2 * bit(me_dp, b)), me_row
        return me_dp, me_row + 2 * (2**b) * (1 - 2 * bit(me_q, b))

    steps_all = [("core", 0)] + [("dp", b) for b in range(bits_of(dp))]
    steps_all += [("q", b) for b in range(q_bits)]
    barrier = pltpu.get_barrier_semaphore()
    for step in steps_all:
        pl.semaphore_signal(barrier, inc=1, device_id=partner(step), device_id_type=MESH)
    pl.semaphore_wait(barrier, len(steps_all))

    counter = [0]

    def push(src, dst, step):
        at = counter[0]
        counter[0] += 1
        copy = pltpu.make_async_remote_copy(
            src_ref=src, dst_ref=dst, send_sem=send_sem.at[at], recv_sem=recv_sem.at[at],
            device_id=partner(step), device_id_type=MESH,
        )
        copy.start()
        return copy

    state = []
    free = list(recvs)
    started = []
    for at, (source, first, rows, steps) in enumerate(layout):
        acc = accs[at]
        rows_at = pl.ds(first, rows)
        if source == 0:
            every = (slice(None),) * q_bits
            landing = free.pop(0)
            local = pltpu.make_async_copy(
                partial_ref.at[every + (core, rows_at)], acc, local_sem.at[at]
            )
            copy = push(partial_ref.at[every + (1 - core, rows_at)], landing, ("core", 0))
            started.append(copy)
        else:
            landing, copy = None, None
            local = pltpu.make_async_copy(summed_ref.at[rows_at], acc, local_sem.at[at])
        local.start()
        state.append(dict(
            acc=acc, number=at, source=source, local=local, copy=copy,
            landing=landing, picked=[None] * (q_bits if source == 0 else 0), off=0, rows=rows,
            steps=list(steps), todo=list(steps),
        ))

    def index_of(item, off, rows):
        picks = tuple(slice(None) if p is None else p for p in item["picked"])
        return picks + (pl.ds(pl.multiple_of(off, 16), rows),)

    def add_landing(item):
        acc, landing = item["acc"], item["landing"]
        rows = item["rows"]
        picks = index_of(item, 0, 16)[:-1]
        lead = (slice(None),) * (len(landing.shape) - 2)

        def body(i, carry):
            own = picks + (pl.ds(pl.multiple_of(item["off"] + i * 16, 16), 16),)
            other = lead + (pl.ds(pl.multiple_of(i * 16, 16), 16),)
            acc[own] = (acc[own].astype(f32) + landing[other].astype(f32)).astype(bf16)
            return carry

        lax.fori_loop(0, rows // 16, body, 0)

    def send_next(item):
        kind, b = item["todo"].pop(0)
        landing = free.pop(0)
        if kind == "dp":
            half = item["rows"] // 2
            mine = bit(me_dp, b)
            src = item["acc"].at[index_of(item, item["off"] + (1 - mine) * half, half)]
            item["copy"] = push(src, landing, (kind, b))
            item["off"] = item["off"] + mine * half
            item["rows"] = half
        else:
            mine = bit(me_q, b)
            place = q_bits - 1 - b
            item["picked"][place] = 1 - mine
            src = item["acc"].at[index_of(item, item["off"], item["rows"])]
            item["copy"] = push(src, landing, (kind, b))
            item["picked"][place] = mine
        started.append(item["copy"])
        item["landing"] = landing

    for item in state:
        if item["source"] == 1:
            item["local"].wait()
            send_next(item)
    busy = [item for item in state if item["source"] == 0] + [
        item for item in state if item["source"] == 1
    ]
    gathering = []
    while busy:
        for item in list(busy):
            if item["local"] is not None and item["source"] == 0:
                item["local"].wait()
                item["local"] = None
            item["copy"].wait_recv()
            add_landing(item)
            if item["todo"]:
                send_next(item)
            else:
                busy = [other for other in busy if other is not item]
                base = item["base"] = layout_base(layout, item["number"])
                picks = index_of(item, item["off"], item["rows"])
                out_ref[pl.ds(pl.multiple_of(base + item["off"], 16), item["rows"]), :] = item["acc"][picks]
                item["back"] = [s for s in item["steps"] if s[0] == "dp"][::-1]
                gather_next(item, out_ref, push, bit, me_dp, started)
                gathering.append(item)
    while gathering:
        for item in list(gathering):
            item["copy"].wait_recv()
            kind, b = item["back"].pop(0)
            item["off"] = item["off"] - bit(me_dp, b) * item["rows"]
            item["rows"] *= 2
            if item["back"]:
                gather_next(item, out_ref, push, bit, me_dp, started)
            else:
                gathering = [other for other in gathering if other is not item]
    for copy in started:
        copy.wait_send()


def layout_base(layout, at):
    return sum(item[2] for item in layout[:at])


def gather_next(item, out_ref, push, bit, me_dp, started):
    at = pl.ds(pl.multiple_of(item["base"] + item["off"], 16), item["rows"])
    item["copy"] = push(out_ref.at[at], out_ref.at[at], item["back"][0])
    started.append(item["copy"])


def reduce_everything(partial, summed, dp, row, orders, summed_orders):
    q_bits, dp_bits = bits_of(row // 2), bits_of(dp)
    layout = [
        (0, first, rows, stream_steps(rows, order, dp_bits, q_bits))
        for first, rows, order in plan_streams(partial.shape[1], dp, orders)
    ] + [
        (1, first, rows, stream_steps(rows, order, dp_bits, 0))
        for first, rows, order in plan_streams(summed.shape[0], dp, summed_orders)
    ]
    accs, recvs = [], []
    for source, _, rows, steps in layout:
        lead = (2,) * (q_bits if source == 0 else 0)
        accs.append(pltpu.VMEM(lead + (rows, D), bf16))
    for source, _, rows, steps in layout:
        if source == 0:
            recvs.append((0, pltpu.VMEM((2,) * q_bits + (rows, D), bf16)))
    walk = [
        dict(rows=rows, lead=q_bits if source == 0 else 0, todo=list(steps), source=source)
        for source, _, rows, steps in layout
    ]

    def landing(item):
        kind, _ = item["todo"].pop(0)
        if kind == "dp":
            item["rows"] //= 2
        else:
            item["lead"] -= 1
        recvs.append((1, pltpu.VMEM((2,) * item["lead"] + (item["rows"], D), bf16)))

    for item in walk:
        if item["source"] == 1:
            landing(item)
    busy = [i for i in walk if i["source"] == 0] + [i for i in walk if i["source"] == 1]
    while busy:
        for item in list(busy):
            if item["todo"]:
                landing(item)
            else:
                busy.remove(item)
    recvs = [spec for _, spec in recvs]
    n_copies = len(recvs) + len(layout) * dp_bits
    rows_out = sum(item[2] for item in layout)
    view = (2,) * q_bits + (2,) + partial.shape[1:]
    return pl.pallas_call(
        functools.partial(reduce_kernel, layout, dp, row),
        out_shape=jax.ShapeDtypeStruct((rows_out, D), bf16),
        in_specs=[pl.BlockSpec(memory_space=pl.ANY)] * 2,
        out_specs=pl.BlockSpec(memory_space=pltpu.VMEM),
        scratch_shapes=accs + recvs + [
            pltpu.SemaphoreType.DMA((n_copies,)),
            pltpu.SemaphoreType.DMA((n_copies,)),
            pltpu.SemaphoreType.DMA((len(layout),)),
        ],
        compiler_params=pltpu.CompilerParams(
            collective_id=3, has_side_effects=True, vmem_limit_bytes=VMEM_ASK
        ),
        name="reduce_everything",
    )(partial.reshape(view), summed)


def row_of(lead, me_row):
    return lead + (me_row,)


def greet_row(row):
    me_dp, me_row = lax.axis_index("dp"), lax.axis_index("row")
    barrier = pltpu.get_barrier_semaphore()
    for ahead in range(1, row):
        pl.semaphore_signal(
            barrier, inc=1, device_id=(me_dp, lax.rem(me_row + ahead, row)), device_id_type=MESH
        )
    pl.semaphore_wait(barrier, row - 1)


def edge_copies(cells, above, below, send_sem, recv_sem, row):
    me_dp, me_row = lax.axis_index("dp"), lax.axis_index("row")
    here = cells.shape[1]
    onward = pltpu.make_async_remote_copy(
        src_ref=cells.at[:, here - 1], dst_ref=above, send_sem=send_sem.at[0],
        recv_sem=recv_sem.at[0], device_id=(me_dp, lax.rem(me_row + 1, row)), device_id_type=MESH,
    )
    back = pltpu.make_async_remote_copy(
        src_ref=cells.at[:, 0], dst_ref=below, send_sem=send_sem.at[1],
        recv_sem=recv_sem.at[1], device_id=(me_dp, lax.rem(me_row + row - 1, row)),
        device_id_type=MESH,
    )
    return onward, back


def start_edges(copies):
    for copy in copies:
        copy.start()


def end_edges(copies):
    for copy in copies:
        copy.wait_send()
        copy.wait_recv()


def put_wide(wide, frame, first, cells):
    column = lax.broadcasted_iota(jnp.int32, cells.shape, 0) % IMG
    cells = cells.astype(f32)
    count = cells.shape[0]
    left = jnp.where(column == 0, 0.0, pltpu.roll(cells, 1, 0))
    right = jnp.where(column == IMG - 1, 0.0, pltpu.roll(cells, count - 1, 0))
    at = pl.ds(first, count)
    wide[frame, at, 0:C] = left.astype(bf16)
    wide[frame, at, C : 2 * C] = cells.astype(bf16)
    wide[frame, at, 2 * C : 3 * C] = right.astype(bf16)


def put_edges(wide, above, below, here, row):
    me_row = lax.axis_index("row")
    keep_above = jnp.where(me_row > 0, 1.0, 0.0)
    keep_below = jnp.where(me_row < row - 1, 1.0, 0.0)
    for frame in range(wide.shape[0]):
        put_wide(wide, frame, 0, above[frame].astype(f32) * keep_above)
        put_wide(wide, frame, (here + 1) * IMG, below[frame].astype(f32) * keep_below)


def conv_forward_kernel(
    row, frames_ref, taps_ref, bias_ref, gain_ref, shift_ref,
    pre_ref, wide_ref, every_ref,
    above_s, below_s, pool_s, edge_send, edge_recv, send_sem, recv_sem,
):
    me_dp, me_row = lax.axis_index("dp"), lax.axis_index("row")
    core, me_q, places = lax.rem(me_row, 2), me_row // 2, row // 2
    count, here = frames_ref.shape[0], frames_ref.shape[1]
    greet_row(row)
    edges = edge_copies(frames_ref, above_s, below_s, edge_send, edge_recv, row)
    start_edges(edges)
    for frame in range(count):
        put_wide(wide_ref, frame, IMG, frames_ref[frame].reshape(here * IMG, C))
    end_edges(edges)
    put_edges(wide_ref, above_s, below_s, here, row)
    tile = POOL * IMG
    for frame in range(count):
        for part in range(here // POOL):
            first = part * tile
            pre = bias_ref[...] + dot_nn(wide_ref[frame, pl.ds(first, tile), :], taps_ref[0])
            pre += dot_nn(wide_ref[frame, pl.ds(first + IMG, tile), :], taps_ref[1])
            pre += dot_nn(wide_ref[frame, pl.ds(first + 2 * IMG, tile), :], taps_ref[2])
            pre_ref[frame, pl.ds(first, tile), :] = pre
            active, _ = gelu_and_slope(pre)
            unit, _ = normalized(active)
            normed = unit * gain_ref[...] + shift_ref[...]
            lines = normed.reshape(POOL, IMG, C)
            lines = lines[0] + lines[1] + lines[2] + lines[3]
            cells = IMG // POOL
            for side in range(C // PAIR):
                lanes = slice(side * PAIR, (side + 1) * PAIR)
                pool_s[side] = lines[:, lanes]
                total = pool_s[side, pl.ds(0, cells, stride=POOL), :]
                for at in range(1, POOL):
                    total += pool_s[side, pl.ds(at, cells, stride=POOL), :]
                every_ref[frame, me_row, pl.ds(part * cells, cells), lanes] = (
                    total * (1.0 / (POOL * POOL))
                ).astype(bf16)

    def push(source_row, to_row, at):
        copy = pltpu.make_async_remote_copy(
            src_ref=every_ref.at[:, source_row], dst_ref=every_ref.at[:, source_row],
            send_sem=send_sem.at[at], recv_sem=recv_sem.at[at], device_id=(me_dp, to_row),
            device_id_type=MESH,
        )
        copy.start()
        return copy

    other = me_row + 1 - 2 * core
    copies = [push(me_row, other, 0)]
    for ahead in range(1, places):
        copies.append(push(me_row, lax.rem(me_q + ahead, places) * 2 + core, ahead))
    for ahead in range(1, places):
        copies[ahead].wait_recv()
        came = lax.rem(me_q + places - ahead, places) * 2 + core
        copies.append(push(came, other, places - 1 + ahead))
    copies[0].wait_recv()
    for copy in copies[places:]:
        copy.wait_recv()
    for copy in copies:
        copy.wait_send()


def conv_forward(frames, taps, bias, gain, shift, row):
    count, here = frames.shape[0], frames.shape[1]
    keys = (here // POOL) * (IMG // POOL)
    return pl.pallas_call(
        functools.partial(conv_forward_kernel, row),
        out_shape=(
            jax.ShapeDtypeStruct((count, here * IMG, C), f32),
            jax.ShapeDtypeStruct((count, (here + 2) * IMG, 3 * C), bf16),
            jax.ShapeDtypeStruct((count, row, keys, C), bf16),
        ),
        in_specs=[pl.BlockSpec(memory_space=pltpu.VMEM)] * 5,
        out_specs=[pl.BlockSpec(memory_space=pltpu.VMEM)] * 3,
        scratch_shapes=[
            pltpu.VMEM((count, IMG, C), bf16),
            pltpu.VMEM((count, IMG, C), bf16),
            pltpu.VMEM((C // PAIR, IMG, PAIR), f32),
            pltpu.SemaphoreType.DMA((2,)),
            pltpu.SemaphoreType.DMA((2,)),
            pltpu.SemaphoreType.DMA((row,)),
            pltpu.SemaphoreType.DMA((row,)),
        ],
        compiler_params=pltpu.CompilerParams(
            collective_id=1, has_side_effects=True, vmem_limit_bytes=VMEM_ASK
        ),
        name="conv_forward",
    )(frames, taps.reshape(3, 3 * C, C), bias[None], gain[None], shift[None])


def conv_backward_kernel(
    row, keys_grad_ref, values_grad_ref, key_w_ref, value_w_ref, pre_ref, wide_ref, taps_ref,
    gain_ref,
    frames_grad_ref, filter_grad_ref, bias_grad_ref, gain_grad_ref, shift_grad_ref,
    part_s, landing_s, sum_s, arrive_s, spread_s, grad_s, grad_t_s, wide_s, above_s, below_s,
    edge_send, edge_recv, send_sem, recv_sem,
):
    me_dp, me_row = lax.axis_index("dp"), lax.axis_index("row")
    core, me_q, places = lax.rem(me_row, 2), me_row // 2, row // 2
    count, here = grad_s.shape[0], grad_s.shape[1]
    keys = part_s.shape[3]
    greet_row(row)
    part = lax.dot_general(
        keys_grad_ref[...], key_w_ref[...], (((0,), (1,)), ((), ())), preferred_element_type=f32
    )
    part += lax.dot_general(
        values_grad_ref[...], value_w_ref[...], (((0,), (1,)), ((), ())), preferred_element_type=f32
    )
    part_s[...] = part.astype(bf16).reshape(count, places, 2, keys, C)

    def push(src, dst, to_row, at):
        copy = pltpu.make_async_remote_copy(
            src_ref=src, dst_ref=dst, send_sem=send_sem.at[at], recv_sem=recv_sem.at[at],
            device_id=(me_dp, to_row), device_id_type=MESH,
        )
        copy.start()
        return copy

    copies = [push(part_s.at[:, :, 1 - core], landing_s, me_row + 1 - 2 * core, 0)]
    copies[0].wait_recv()
    sum_s[...] = (part_s[:, :, core].astype(f32) + landing_s[...].astype(f32)).astype(bf16)
    for ahead in range(1, places):
        to = lax.rem(me_q + ahead, places)
        copies.append(push(sum_s.at[:, to], arrive_s.at[ahead - 1], to * 2 + core, ahead))
    for copy in copies[1:]:
        copy.wait_recv()
    pooled = sum_s[:, me_q].astype(f32)
    for ahead in range(1, places):
        pooled += arrive_s[ahead - 1].astype(f32)
    pooled = pooled * (1.0 / (POOL * POOL))

    tile = POOL * IMG
    cells = IMG // POOL
    bias_grad = jnp.zeros((1, C), f32)
    gain_grad = jnp.zeros((1, C), f32)
    shift_grad = jnp.zeros((1, C), f32)
    for frame in range(count):
        for part in range(here // POOL):
            for side in range(C // PAIR):
                own = pooled[
                    frame, part * cells : (part + 1) * cells, side * PAIR : (side + 1) * PAIR
                ]
                for at in range(POOL):
                    spread_s[side, pl.ds(at, cells, stride=POOL), :] = own
            line = jnp.concatenate([spread_s[side] for side in range(C // PAIR)], 1)
            back = jnp.broadcast_to(line[None], (POOL, IMG, C)).reshape(tile, C)
            active, slope = gelu_and_slope(pre_ref[frame, pl.ds(part * tile, tile), :])
            unit, spread = normalized(active)
            grad, one, two = norm_back(unit, spread, gain_ref[...], back)
            gain_grad += one[None]
            shift_grad += two[None]
            grad = (slope * grad).astype(bf16)
            bias_grad += jnp.sum(grad.astype(f32), 0, keepdims=True)
            grad_s[frame, pl.ds(part * POOL, POOL)] = grad.reshape(POOL, IMG, C)
    bias_grad_ref[...] = bias_grad
    gain_grad_ref[...] = gain_grad
    shift_grad_ref[...] = shift_grad
    edges = edge_copies(grad_s, above_s, below_s, edge_send, edge_recv, row)
    start_edges(edges)
    for frame in range(count):
        cells_here = grad_s[frame].reshape(here * IMG, C)
        put_wide(wide_s, frame, IMG, cells_here)
        grad_t_s[frame] = cells_here.T
    for dy in range(3):
        total = None
        for frame in range(count):
            piece = dot_nn(grad_t_s[frame], wide_ref[frame, pl.ds(dy * IMG, here * IMG), :])
            total = piece if total is None else total + piece
        filter_grad_ref[dy] = total.astype(bf16)
    end_edges(edges)
    put_edges(wide_s, above_s, below_s, here, row)
    for frame in range(count):
        for part in range(here // POOL):
            total = None
            for tap in range(9):
                dy, dx = tap // 3, tap % 3
                window = wide_s[frame, pl.ds(part * tile + dy * IMG, tile), dx * C : (dx + 1) * C]
                piece = dot_nt(window, taps_ref[8 - tap])
                total = piece if total is None else total + piece
            frames_grad_ref[frame, pl.ds(part * tile, tile), :] = total
    for copy in copies:
        copy.wait_send()


def conv_backward(keys_grad_t, values_grad_t, key_w, value_w, pre, wide, taps, gain, row):
    count = pre.shape[0]
    here = pre.shape[1] // IMG
    keys = (here // POOL) * (IMG // POOL)
    return pl.pallas_call(
        functools.partial(conv_backward_kernel, row),
        out_shape=(
            jax.ShapeDtypeStruct(pre.shape, f32),
            jax.ShapeDtypeStruct((3, C, 3 * C), bf16),
            jax.ShapeDtypeStruct((1, C), f32),
            jax.ShapeDtypeStruct((1, C), f32),
            jax.ShapeDtypeStruct((1, C), f32),
        ),
        in_specs=[pl.BlockSpec(memory_space=pltpu.VMEM)] * 8,
        out_specs=[pl.BlockSpec(memory_space=pltpu.VMEM)] * 5,
        scratch_shapes=[
            pltpu.VMEM((count, row // 2, 2, keys, C), bf16),
            pltpu.VMEM((count, row // 2, keys, C), bf16),
            pltpu.VMEM((count, row // 2, keys, C), bf16),
            pltpu.VMEM((row // 2 - 1, count, keys, C), bf16),
            pltpu.VMEM((C // PAIR, IMG, PAIR), f32),
            pltpu.VMEM((count, here, IMG, C), bf16),
            pltpu.VMEM((count, C, here * IMG), bf16),
            pltpu.VMEM((count, (here + 2) * IMG, 3 * C), bf16),
            pltpu.VMEM((count, IMG, C), bf16),
            pltpu.VMEM((count, IMG, C), bf16),
            pltpu.SemaphoreType.DMA((2,)),
            pltpu.SemaphoreType.DMA((2,)),
            pltpu.SemaphoreType.DMA((row,)),
            pltpu.SemaphoreType.DMA((row,)),
        ],
        compiler_params=pltpu.CompilerParams(
            collective_id=2, has_side_effects=True, vmem_limit_bytes=VMEM_ASK
        ),
        name="conv_backward",
    )(keys_grad_t, values_grad_t, key_w, value_w, pre, wide, taps, gain[None])


def fast_dot(left, right):
    return jnp.dot(left, right, preferred_element_type=f32)


def shared_rows(matrix, count):
    return matrix.reshape(count, matrix.shape[0] // count, matrix.shape[1])


def on_device(
    frames, tokens, segment_ids, clip_frame, filter_weight, filter_bias, context_gain,
    context_shift, cross_query, cross_key, cross_value, cross_output, first_gain, first_shift,
    self_project, self_output, second_gain, second_shift, up_weight, up_bias, down_weight, cotangent,
):
    shares = lax.axis_size("row")
    x = tokens[0]
    segments = segment_ids[0]
    clip_frames = clip_frame[0]
    out_grad = cotangent[0]
    tags = segment_tags(segments)
    key_tag = key_tags(segments)
    first_blocks = first_block_table(segments)

    pre_act, wide, everyone = conv_forward(
        frames, filter_weight, filter_bias, context_gain, context_shift, shares
    )
    everyone = everyone.reshape(-1, C)
    cross_q = fast_dot(x, cross_query).astype(bf16)
    cross_mixed, cross_extra = cross_forward(
        segments, clip_frames, cross_q, everyone, cross_key, cross_value, tags
    )
    middle = x.astype(f32) + fast_dot(cross_mixed, cross_output)
    first_unit, first_spread = normalized(middle)
    first_normed = (first_unit * first_gain + first_shift).astype(bf16)
    packed = fast_dot(first_normed, self_project).astype(bf16)
    self_mixed, self_extra = self_forward(first_blocks, packed, tags, key_tag)
    (
        output, second_grad, second_low, self_mixed_grad, join_grad, second_gain_grad,
        second_shift_grad, up_bias_grad, chunk_a,
    ) = feed_forward(
        middle, self_mixed, self_output, second_gain, second_shift, up_weight, up_bias, down_weight,
        out_grad, shares,
    )
    share_a = lax.psum_scatter(chunk_a, "row", scatter_dimension=0, tiled=False)
    query_grad, key_grad, value_grad = self_backward(
        first_blocks, packed, key_tag, self_extra, self_mixed, self_mixed_grad
    )
    (
        middle_grad, cross_mixed_grad, project_grad, cross_join_grad, first_gain_grad,
        first_shift_grad,
    ) = project_back(
        query_grad, key_grad, value_grad, self_project, middle, second_grad, first_gain, first_shift,
        cross_output, cross_mixed,
    )
    cross_q_grad, keys_grad_t, values_grad_t = cross_backward(
        segments, clip_frames, cross_q, everyone, cross_key, cross_value, cross_extra, cross_mixed,
        cross_mixed_grad,
    )
    tokens_grad = middle_grad + dot_nt(cross_q_grad, cross_query)

    frames_grad, filter_grad, filter_bias_grad, context_gain_grad, context_shift_grad = conv_backward(
        keys_grad_t, values_grad_t, cross_key, cross_value, pre_act, wide, filter_weight,
        context_gain, shares,
    )
    filter_pieces = [shared_rows(filter_grad[dy], shares) for dy in range(3)]
    small = jnp.concatenate(
        [
            item.astype(bf16).reshape(shares, -1)
            for item in (
                first_gain_grad, first_shift_grad, second_gain_grad, second_shift_grad,
                up_bias_grad, filter_bias_grad, context_gain_grad, context_shift_grad,
            )
        ],
        1,
    )
    small = jnp.pad(small, ((0, 0), (0, 16 * D - small.shape[1]))).reshape(shares, 16, D)
    key_pieces = [
        jnp.pad(
            fast_dot(grad_t, everyone).astype(bf16).reshape(shares, D // shares, C),
            ((0, 0), (0, 0), (0, 0)),
        )
        for grad_t in (keys_grad_t, values_grad_t)
    ]
    key_pieces = jnp.concatenate(
        key_pieces + [jnp.zeros_like(key_pieces[0])], 2
    )
    chunk = [
        shared_rows(project_grad, shares),
        shared_rows(join_grad, shares),
        shared_rows(cross_join_grad, shares),
        shared_rows(dot_tn(cross_q_grad, x).astype(bf16), shares),
        key_pieces,
        *filter_pieces,
        small,
    ]
    used = sum(item.shape[1] for item in chunk)
    unit = 16 * lax.axis_size("dp")
    spare = -used % unit
    if spare:
        chunk.append(jnp.zeros((shares, spare, D), bf16))
    reduced = reduce_everything(
        jnp.concatenate(chunk, 1), share_a, lax.axis_size("dp"), shares,
        ("up", "down", "q_up") * 2 + ("up",), ("up", "down"),
    )
    share_b, share_c = reduced[: 4 * D // shares], reduced[4 * D // shares : used]
    share_a = reduced[used + spare :]

    wide_part, model_part, own_part = 3072 // shares, D // shares, C // shares
    up_grad = share_a[:wide_part].astype(f32).T
    down_grad = jnp.concatenate(
        [
            share_a[wide_part + part * model_part : wide_part + (part + 1) * model_part].T
            for part in range(4)
        ],
        0,
    ).astype(f32)
    project_grad = share_b[: 3 * model_part].astype(f32).T
    self_output_grad = share_b[3 * model_part :].astype(f32).T
    at = 0

    def take(count):
        nonlocal at
        at += count
        return share_c[at - count : at].astype(f32)

    cross_output_grad = take(model_part).T
    cross_query_grad = take(model_part).T
    both = take(model_part)
    cross_key_grad = both[:, :C].T
    cross_value_grad = both[:, C : 2 * C].T
    filter_grad = jnp.concatenate(
        [jnp.transpose(take(own_part).reshape(own_part, 3, C), (1, 2, 0)) for _ in range(3)], 0
    )
    flat = take(16).reshape(-1)
    sizes = [model_part] * 4 + [wide_part] + [own_part] * 3
    ends = [sum(sizes[: i + 1]) for i in range(len(sizes))]
    vectors = [flat[e - s : e] for e, s in zip(ends, sizes)]
    return (
        middle[None],
        output[None],
        tokens_grad[None],
        frames_grad.reshape(frames.shape),
        filter_grad,
        vectors[5],
        vectors[6],
        vectors[7],
        cross_query_grad,
        cross_key_grad,
        cross_value_grad,
        cross_output_grad,
        vectors[0],
        vectors[1],
        project_grad,
        self_output_grad,
        vectors[2],
        vectors[3],
        up_grad,
        vectors[4],
        down_grad,
    )


def solution(mesh):
    whole = P()
    by_row = P(("dp", "row"), None, None)
    in_specs = (
        P("dp", "row", None, None),
        by_row,
        P(("dp", "row"), None),
        P(("dp", "row"), None),
    ) + (whole,) * 17 + (by_row,)
    columns = P(None, "row")
    vector = P("row")
    out_specs = (
        by_row, by_row, by_row, P("dp", "row", None, None), P(None, None, "row"), vector, vector,
        vector, columns, columns, columns, columns, vector, vector, columns, columns, vector, vector,
        columns, vector, columns,
    )
    return jax.shard_map(
        on_device, mesh=mesh, in_specs=in_specs, out_specs=out_specs, check_vma=False
    )
```

time: 1640 us -> 399 us (0.24)
  waiting for transfers between devices: 638 us -> 0.02 us
  matrix products: 487 us -> 17.3 us
  Pallas kernels: 0 us -> 307 us
  local copies, waits for them, and re-layouts: 250 us -> 42.4 us
  other arithmetic: 216 us -> 12.6 us
  loops' own time: 17.9 us -> 0 us
    dot_general x79 -> x7, matrix products: 487 us -> 17.3 us  [the longest x5 12.7 us: fast_dot(): return jnp.dot(left, right, preferred_element_type=f32)]
    reduce_scatter x10 -> x1, waiting for transfers between devices: 336 us -> 0.01 us  [on_device(): share_a = lax.psum_scatter(chunk_a, 'row', scatter_dimension=0, tiled=False)]
    pallas_call x0 -> x9, Pallas kernels: none -> 307 us  [the longest x1 73.2 us: reduce_everything(): pl.pallas_call(functools.partial(reduce_kernel, layout, dp, row), out_sha...]
    unnamed x32 -> x1, waiting for transfers between devices: 161 us -> 0.02 us
    psum x2 -> x0, waiting for transfers between devices: 108 us -> none  [the longest x1 68.6 us: on_device(): lax.psum(shares[0].astype(jnp.bfloat16), 'dp').astype(jnp.float32)]
    convert_element_type x16 -> x10, other arithmetic: 108 us -> 2.95 us  [the longest x8 1.56 us: on_device(): item.astype(bf16).reshape(shares, -1)]
    reduce_sum x17 -> x3, other arithmetic: 73.7 us -> 1.56 us  [the longest x1 0.9 us: first_block_table(): jnp.sum((segment_row[:, None] < clips[None, :]).astype(jnp.int32), 0)]
    unnamed x219 -> x108, local copies, waits for them, and re-layouts: 79.8 us -> 30.1 us
  transfers between devices with their start and end apart: 27 -> 1, of which waited for: 20 -> 0; matrix products, arithmetic and copies ran while one was open for 13% -> 6% of each run, Pallas kernels for 0% -> 30%
where the time goes in v1:
time: 399 us; the launch traced here: 394 us
  Pallas kernels  307 us (77%)
  local copies, waits for them, and re-layouts  42.4 us (11%)
  matrix products  17.3 us (4%)
  between operations  15.1 us (4%)
  other arithmetic  12.6 us (3%)
    pallas_call x1, Pallas kernels, reduce_everything(): pl.pallas_call(functools.partial(reduce_kernel, layout, dp, row), out_sha...  73.2 us
    pallas_call x1, Pallas kernels, conv_backward(): pl.pallas_call(functools.partial(conv_backward_kernel, row), out_shape=(j...  49.6 us
    pallas_call x1, Pallas kernels, feed_forward(): pl.pallas_call(feed_forward_kernel, out_shape=(jax.ShapeDtypeStruct((rows...  47.7 us
    unnamed x108, local copies, waits for them, and re-layouts  30.1 us
    pallas_call x1, Pallas kernels, cross_backward(): pl.pallas_call(cross_backward_kernel, out_shape=(jax.ShapeDtypeStruct((ro...  27.3 us
    pallas_call x1, Pallas kernels, cross_forward(): pl.pallas_call(cross_forward_kernel, out_shape=(jax.ShapeDtypeStruct((row...  25.9 us
    pallas_call x1, Pallas kernels, self_backward(): pl.pallas_call(self_backward_kernel, out_shape=(jax.ShapeDtypeStruct((row...  22.1 us
    pallas_call x1, Pallas kernels, conv_forward(): pl.pallas_call(functools.partial(conv_forward_kernel, row), out_shape=(ja...  21.5 us
  transfers between devices with their start and end apart: 1, of which 0 were waited for; matrix products, arithmetic and copies ran while one was open for 6% of the time, Pallas kernels for 30%

profile of v1, /device:TPU:0, one launch (start us, length us, event | category | flops | bytes accessed | tf_op | source)
XLA Modules:
  0.0 394.4 jit_solution(16292659284763105707)
XLA Ops:
  7.3 0.9 convert_reduce_fusion
  8.1 0.8 slice.101
  10.1 1.3 broadcast_in_dim.86.gain_ref
  11.4 1.3 broadcast_in_dim.87.shift_ref
  12.7 0.9 copy.52.col_ref
  13.7 4.1 %convolution_convert_fusion.1.q_ref = bf16[1024,768]{1,0:T(8,128)(2,1)} fusion(bf16[768,768]{1,0:T(8,128)(2,1)S(1)} %copy-done, bf16[1,1024,768]{2,1,0:T(8,128)(2,1)} %param.23), kind=kOutput, calls=%fused_computation.5 | convolution fusion | flops 1208745984 | bytes 4325376 | tf_op jit(solution)/shard_map/dot_general | solution.py:1184
  18.2 21.5 %conv_forward.1 = (f32[4,512,256]{2,1,0:T(8,128)S(1)}, bf16[4,640,768]{2,1,0:T(8,128)(2,1)}, bf16[4,8,32,256]{3,2,1,0:T(8,128)(2,1)S(1)}) custom-call(bf16[4,8,64,256]{3,2,1,0:T(8,128)(2,1)S(1)} %copy-done.11, bf16[3,768,256]{2,1,0:T(8,128)(2,1)S(1)} %bitcast.72, f32[1,256]{1,0:T(1,128)S(1)} %bitcast.82, f32[1,256]{1,0:T(1,128)S(1)} %bitcast.80, ...), custom_call_target="tpu_custom_call" | custom-call | tf_op jit(solution)/shard_map/conv_forward/pallas_call | solution.py:1026
  39.7 1.3 copy-done.3
  41.1 25.9 %cross_forward.1 = (bf16[1024,768]{1,0:T(8,128)(2,1)S(1)}, bf16[1024,768]{1,0:T(8,128)(2,1)S(1)}) custom-call(s32[1024]{0:T(1024)S(1)} %bitcast.78, s32[4]{0:T(128)S(1)} %bitcast.88, bf16[1024,768]{1,0:T(8,128)(2,1)} %convolution_convert_fusion.1.q_ref, bf16[1024,256]{1,0:T(8,128)(2,1)S(1)} %bitcast.84, bf16[256,768]{1,0:T(8,128)(2,1)S(1)} %copy-done.12, ...), custom_call_target="tpu_custom_call" | custom-call | flops 12000000000 | bytes 8000000 | tf_op jit(solution)/shard_map/cross_forward/pallas_call | solution.py:117
  67.1 1.5 fusion.14
  69.2 2.1 copy-done.44
  71.3 5.9 %convolution_convert_fusion.q_ref.k_ref.v_ref = bf16[1024,2304]{1,0:T(8,128)(2,1)} fusion(bf16[768,2304]{1,0:T(8,128)(2,1)S(1)} %copy-done.44, f32[1024,768]{1,0:T(8,128)S(1)} %get-tuple-element.174.middle_ref, f32[768]{0:T(1024)S(1)} %copy-done.38, f32[768]{0:T(1024)S(1)} %copy-done.37, f32[1024]{0:T(1024)S(1)} %add_rsqrt_fusion, ...), kind=kOutput, calls=%fused_computation | convolution fusion | flops 3630170112 | bytes 11417600 | tf_op jit(solution)/shard_map/dot_general | solution.py:1184
  77.2 20.6 %self_forward.1 = (bf16[1024,768]{1,0:T(8,128)(2,1)S(1)}, bf16[1024,768]{1,0:T(8,128)(2,1)S(1)}) custom-call(s32[4]{0:T(128)S(1)} %and_select_fusion.first_ref, bf16[1024,2304]{1,0:T(8,128)(2,1)} %convolution_convert_fusion.q_ref.k_ref.v_ref, bf16[1024,2304]{1,0:T(8,128)(2,1)} %convolution_convert_fusion.q_ref.k_ref.v_ref, ...), custom_call_target="tpu_custom_call" | custom-call | flops 12000000000 | bytes 8000000 | tf_op jit(solution)/shard_map/self_forward/pallas_call | solution.py:212
  97.9 1.1 copy-done.28
  99.0 1.2 copy-done.29
  100.2 47.7 %feed_forward.1 = (f32[1024,768]{1,0:T(8,128)}, f32[1024,768]{1,0:T(8,128)}, bf16[1024,768]{1,0:T(8,128)(2,1)}, bf16[1024,768]{1,0:T(8,128)(2,1)}, bf16[768,768]...) custom-call(f32[1024,768]{1,0:T(8,128)} %copy-done.31, ...), custom_call_target="tpu_custom_call" | custom-call | flops 33999998976 | bytes 40000000 | tf_op jit(solution)/shard_map/feed_forward/pallas_call | solution.py:556
  150.6 22.1 %self_backward.1 = (bf16[1024,768]{1,0:T(8,128)(2,1)S(1)}, bf16[1024,768]{1,0:T(8,128)(2,1)S(1)}, bf16[1024,768]{1,0:T(8,128)(2,1)S(1)}) custom-call(s32[4]{0:T(128)S(1)} %and_select_fusion.first_ref, bf16[1024,2304]{1,0:T(8,128)(2,1)} %convolution_convert_fusion.q_ref.k_ref.v_ref, bf16[1024,2304]{1,0:T(8,128)(2,1)} %convolution_convert_fusion.q_ref.k_ref.v_ref, ...), custom_call_target="tpu_custom_call" | custom-call | flops 24000000000 | bytes 16000000 | tf_op jit(solution)/shard_map/self_backward/pallas_call | solution.py:390
  172.8 1.1 copy-done.25
  173.9 1.2 copy-done.26
  175.1 1.1 copy-done.27
  176.2 19.0 %project_back.1 = (f32[1024,768]{1,0:T(8,128)}, bf16[1024,768]{1,0:T(8,128)(2,1)}, bf16[2304,768]{1,0:T(8,128)(2,1)}, bf16[768,768]{1,0:T(8,128)(2,1)}, f32[1,768]{1,0:T(1,128)}, /*index=5*/f32[1,768]{1,0:T(1,128)}) custom-call(bf16[1024,768]{1,0:T(8,128)(2,1)} %copy-done.25, bf16[1024,768]{1,0:T(8,128)(2,1)} %copy-done.26, bf16[1024,768]{1,0:T(8,128)(2,1)} %copy-done.27, ...), custom_call_target="tpu_custom_call" | custom-call | flops 10000000000 | bytes 30000000 | tf_op jit(solution)/shard_map/project_back/pallas_call | solution.py:636
  195.2 27.3 %cross_backward.1 = (bf16[1024,768]{1,0:T(8,128)(2,1)S(1)}, bf16[768,1024]{1,0:T(8,128)(2,1)S(1)}, bf16[768,1024]{1,0:T(8,128)(2,1)S(1)}) custom-call(s32[1024]{0:T(1024)S(1)} %bitcast.79, s32[4]{0:T(128)S(1)} %bitcast.89, bf16[1024,768]{1,0:T(8,128)(2,1)} %convolution_convert_fusion.1.q_ref, bf16[1024,256]{1,0:T(8,128)(2,1)S(1)} %bitcast.85, ...), custom_call_target="tpu_custom_call" | custom-call | flops 24000000000 | bytes 16000000 | tf_op jit(solution)/shard_map/cross_backward/pallas_call | solution.py:306
  222.5 1.1 copy-done.4
  223.7 1.2 copy-done.6
  224.9 49.6 %conv_backward.1 = (f32[4,512,256]{2,1,0:T(8,128)}, bf16[3,256,768]{2,1,0:T(8,128)(2,1)S(1)}, f32[1,256]{1,0:T(1,128)S(1)}, f32[1,256]{1,0:T(1,128)S(1)}, f32[1,256]{1,0:T(1,128)S(1)}) custom-call(bf16[768,1024]{1,0:T(8,128)(2,1)S(1)} %get-tuple-element.67.keys_grad_ref, bf16[768,1024]{1,0:T(8,128)(2,1)} %copy-done.6, bf16[256,768]{1,0:T(8,128)(2,1)S(1)} %copy-done.13, ...), custom_call_target="tpu_custom_call" | custom-call | tf_op jit(solution)/shard_map/conv_backward/pallas_call | solution.py:1149
  276.4 0.8 concatenate.50
  277.3 4.2 %constant_dynamic-update-slice_fusion.7 = bf16[2,2,2,832,768]{4,3,2,1,0:T(8,128)(2,1)} fusion(bf16[2,2,2,288,768]{4,3,2,1,0:T(8,128)(2,1)} %bitcast.90), kind=kLoop, calls=%fused_computation.42 | loop fusion | bytes 7077888
  281.5 1.1 constant_dynamic-update-slice_fusion.6
  283.2 1.1 constant_dynamic-update-slice_fusion.5
  284.4 1.5 fusion.7
  285.9 1.2 constant_dynamic-update-slice_fusion.4
  288.9 1.5 maximum_dynamic-update-slice_fusion
  290.5 0.8 constant_dynamic-update-slice_fusion.3
  291.3 0.8 constant_dynamic-update-slice_fusion.2
  292.1 0.8 constant_dynamic-update-slice_fusion.1
  293.6 0.9 broadcast_dynamic-update-slice_fusion.refs_0_
  294.4 3.1 add_bitcast_fusion
  297.6 1.3 copy-done.10
  298.8 73.2 %reduce_everything.1 = bf16[1600,768]{1,0:T(8,128)(2,1)S(1)} custom-call(bf16[2,2,2,832,768]{4,3,2,1,0:T(8,128)(2,1)} %broadcast_dynamic-update-slice_fusion.refs_0_, bf16[768,768]{1,0:T(8,128)(2,1)S(1)} %bitcast.73), custom_call_target="tpu_custom_call" | custom-call | tf_op jit(solution)/shard_map/reduce_everything/pallas_call | solution.py:882
  372.0 1.4 copy-done.1
  375.2 0.9 fusion.10
  376.1 2.0 convert_bitcast_fusion.1
  378.1 1.1 convert_bitcast_fusion
  379.2 2.3 slice_bitcast_fusion.3
  381.7 0.9 copy.54
  382.6 1.4 copy.55
  384.7 1.1 maximum_convert_fusion
  385.8 1.3 copy.68
  (132 shorter events, 12.8 us)
Async XLA Ops:
  7.2 6.4 %copy-start = (bf16[768,768]{1,0:T(8,128)(2,1)S(1)}, bf16[768,768]{1,0:T(8,128)(2,1)}, u32[]{:S(2)}) copy-start(bf16[768,768]{1,0:T(8,128)(2,1)} %param.30) | copy-start | bytes 3538948
  7.2 290.4 %reduce-scatter.2.cloned.1.call-start = ((), (), s32[]{:S(2)}) async-start(), calls=%async_computation.1 | async-start | bytes 10616832 | tf_op jit(solution)/shard_map/reduce_scatter | solution.py:1225
  13.6 4.2 %copy-start.16 = (s32[1,1024]{1,0:T(1,128)S(1)}, s32[1,1024]{1,0:T(1,128)}, u32[]{:S(2)}) copy-start(s32[1,1024]{1,0:T(1,128)} %param.24) | copy-start | bytes 12292
  13.6 4.2 %copy-start.41 = (s32[128]{0:T(128)S(1)}, s32[128]{0:T(128)}, u32[]{:S(2)}) copy-start(s32[128]{0:T(128)} %and_select_fusion.1) | copy-start | bytes 1540
  13.6 4.2 %copy-start.42 = (pred[128]{0:T(512)(128)(4,1)S(1)}, pred[128]{0:T(512)(128)(4,1)}, u32[]{:S(2)}) copy-start(pred[128]{0:T(512)(128)(4,1)} %get-tuple-element.175) | copy-start | bytes 388
  13.6 4.2 %copy-start.43 = (pred[128]{0:T(512)(128)(4,1)S(1)}, pred[128]{0:T(512)(128)(4,1)}, u32[]{:S(2)}) copy-start(pred[128]{0:T(512)(128)(4,1)} %get-tuple-element.176) | copy-start | bytes 388
  13.7 4.5 %copy-start.2 = (bf16[9,256,256]{2,1,0:T(8,128)(2,1)S(1)}, bf16[9,256,256]{2,1,0:T(8,128)(2,1)}, u32[]{:S(2)}) copy-start(bf16[9,256,256]{2,1,0:T(8,128)(2,1)} %taps_ref.1) | copy-start | bytes 3538948
  13.7 4.5 %copy-start.11 = (bf16[4,8,64,256]{3,2,1,0:T(8,128)(2,1)S(1)}, bf16[4,8,64,256]{3,2,1,0:T(8,128)(2,1)}, u32[]{:S(2)}) copy-start(bf16[4,8,64,256]{3,2,1,0:T(8,128)(2,1)} %frames_ref.1) | copy-start | bytes 3145732
  13.7 4.5 %copy-start.17 = (f32[256]{0:T(256)S(1)}, f32[256]{0:T(256)}, u32[]{:S(2)}) copy-start(f32[256]{0:T(256)} %param.28) | copy-start | bytes 3076
  13.7 4.5 %copy-start.18 = (f32[256]{0:T(256)S(1)}, f32[256]{0:T(256)}, u32[]{:S(2)}) copy-start(f32[256]{0:T(256)} %param.27) | copy-start | bytes 3076
  13.7 4.5 %copy-start.19 = (f32[256]{0:T(256)S(1)}, f32[256]{0:T(256)}, u32[]{:S(2)}) copy-start(f32[256]{0:T(256)} %param.29) | copy-start | bytes 3076
  17.8 23.2 %copy-start.12 = (bf16[256,768]{1,0:T(8,128)(2,1)S(1)}, bf16[256,768]{1,0:T(8,128)(2,1)}, u32[]{:S(2)}) copy-start(bf16[256,768]{1,0:T(8,128)(2,1)} %key_w_ref.5) | copy-start | bytes 1179652
  17.8 23.2 %copy-start.14 = (bf16[256,768]{1,0:T(8,128)(2,1)S(1)}, bf16[256,768]{1,0:T(8,128)(2,1)}, u32[]{:S(2)}) copy-start(bf16[256,768]{1,0:T(8,128)(2,1)} %value_w_ref.5) | copy-start | bytes 1179652
  17.8 23.2 %copy-start.23 = (s32[1,4]{1,0:T(1,128)S(1)}, s32[1,4]{1,0:T(1,128)}, u32[]{:S(2)}) copy-start(s32[1,4]{1,0:T(1,128)} %param.25) | copy-start | bytes 52
  39.7 1.3 copy-start.3
  41.0 26.0 %copy-start.20 = (bf16[4,8,32,256]{3,2,1,0:T(8,128)(2,1)}, bf16[4,8,32,256]{3,2,1,0:T(8,128)(2,1)S(1)}, u32[]{:S(2)}) copy-start(bf16[4,8,32,256]{3,2,1,0:T(8,128)(2,1)S(1)} %get-tuple-element.53) | copy-start | bytes 1572868
  41.1 26.0 %copy-start.45 = (bf16[1,1024,768]{2,1,0:T(8,128)(2,1)S(1)}, bf16[1,1024,768]{2,1,0:T(8,128)(2,1)}, u32[]{:S(2)}) copy-start(bf16[1,1024,768]{2,1,0:T(8,128)(2,1)} %param.23) | copy-start | bytes 4718596
  41.1 26.0 %copy-start.47 = (bf16[768,768]{1,0:T(8,128)(2,1)S(1)}, bf16[768,768]{1,0:T(8,128)(2,1)}, u32[]{:S(2)}) copy-start(bf16[768,768]{1,0:T(8,128)(2,1)} %join_ref.3) | copy-start | bytes 3538948
  67.0 1.6 copy-start.24
  67.1 1.7 copy-start.30
  67.1 4.3 %copy-start.44 = (bf16[768,2304]{1,0:T(8,128)(2,1)S(1)}, bf16[768,2304]{1,0:T(8,128)(2,1)}, u32[]{:S(2)}) copy-start(bf16[768,2304]{1,0:T(8,128)(2,1)} %project_ref.1) | copy-start | bytes 10616836
  68.7 8.5 %copy-start.31 = (f32[1024,768]{1,0:T(8,128)}, f32[1024,768]{1,0:T(8,128)S(1)}, u32[]{:S(2)}) copy-start(f32[1024,768]{1,0:T(8,128)S(1)} %get-tuple-element.174.middle_ref) | copy-start | bytes 9437188
  68.7 2.6 copy-start.37
  68.7 2.6 copy-start.38
  97.9 1.2 copy-start.28
  99.0 1.2 copy-start.29
  147.9 1.2 copy-start.40
  147.9 1.3 copy-start.39
  147.9 2.0 copy-start.36
  172.8 1.1 copy-start.25
  173.9 1.2 copy-start.26
  176.2 19.0 %copy-start.15 = (bf16[256,768]{1,0:T(8,128)(2,1)S(1)}, bf16[256,768]{1,0:T(8,128)(2,1)}, u32[]{:S(2)}) copy-start(bf16[256,768]{1,0:T(8,128)(2,1)} %value_w_ref.5) | copy-start | bytes 1179652
  176.2 19.0 %copy-start.21 = (bf16[4,8,32,256]{3,2,1,0:T(8,128)(2,1)S(1)}, bf16[4,8,32,256]{3,2,1,0:T(8,128)(2,1)}, u32[]{:S(2)}) copy-start(bf16[4,8,32,256]{3,2,1,0:T(8,128)(2,1)} %copy-done.20) | copy-start | bytes 1572868
  195.2 29.7 %copy-start.13 = (bf16[256,768]{1,0:T(8,128)(2,1)S(1)}, bf16[256,768]{1,0:T(8,128)(2,1)}, u32[]{:S(2)}) copy-start(bf16[256,768]{1,0:T(8,128)(2,1)} %key_w_ref.5) | copy-start | bytes 1179652
  222.5 1.1 copy-start.4
  223.7 1.2 copy-start.6
  224.9 49.6 %copy-start.8 = (bf16[768,1024]{1,0:T(8,128)(2,1)}, bf16[768,1024]{1,0:T(8,128)(2,1)S(1)}, u32[]{:S(2)}) copy-start(bf16[768,1024]{1,0:T(8,128)(2,1)S(1)} %get-tuple-element.67.keys_grad_ref) | copy-start | bytes 4718596
  277.3 4.2 %copy-start.34 = (bf16[768,768]{1,0:T(8,128)(2,1)S(1)}, bf16[768,768]{1,0:T(8,128)(2,1)}, u32[]{:S(2)}) copy-start(bf16[768,768]{1,0:T(8,128)(2,1)} %get-tuple-element.73) | copy-start | bytes 3538948
  281.5 1.7 copy-start.35
  281.5 2.8 copy-start.5
  281.5 2.8 copy-start.46
  285.8 1.8 copy-start.9
  285.8 1.9 copy-start.22
  285.9 2.5 copy-start.7
  290.5 3.9 copy-start.32
  297.6 1.3 copy-start.10
  372.0 1.4 copy-start.1
  384.0 1.8 copy-start.33
  (1 other events, 1.1 us)
Sparse Core Ops, SparseCore 0:
  148.1 112.9 reduce-scatter.1
